TPU v7x, 512 devices: a whole 4x8x8 slice. The times are simulated.
512 devices in a mesh: head: 8 (over y), ctx: 16 (over z, core), rep: 4 (over x).
Axes of the slice: x: 4, y: 8, z: 8, core: 2. Of those that a mesh axis runs over, the one named last changes fastest.
Arguments:
- inputs: bfloat16 [4, 8192, 8192], P('rep', 'ctx', 'head'), may hold values from -6 to 6
- b_proj: bfloat16 [4, 8192, 2048], P('rep', 'ctx', 'head'), may hold values from -0.375 to 0.375
- c_proj: bfloat16 [4, 8192, 2048], P('rep', 'ctx', 'head'), may hold values from -0.375 to 0.375
- log_decay: bfloat16 [4, 128, 8192], P('rep', 'head', 'ctx'), may hold values from -1 to 0
- starts: int32 [4, 8192], P('rep', 'ctx'), may hold values 0 or 1
- counts: int32 [4, 16], P('rep', 'ctx'), may hold values from 0 to 512, as said below
- skip_gain: float32 [128], P('head'), may hold values from 0.5 to 1.5
- readout: bfloat16 [8192], P('head'), may hold values from -0.0625 to 0.0625
Outputs:
- ssd_out: bfloat16 [4, 8192, 8192], P('rep', 'ctx', 'head')
- token_scores: float32 [4, 8192], P('rep', 'ctx')
Inputs may be any that keep to these rules, and one draw needn't show every extreme that they name: `counts`: at each ctx index, the two rows 2q and 2q + 1 (q = 0, 1, ...) together hold live slots in exactly 2 spans, counting ceil(count / 256) for each; one of the two holds all of them and the other none.
All inputs are finite; a program needn't handle non-finite values. No bound on the sum of `starts` on one device may be relied on, other than what follows from the above.
Results may differ from a plain program's by a relative error of at most 0.0056.
Values may be sent and summed in bfloat16 or wider, within the bound.
A program may use at most 64 MiB of HBM per device.

v0:
```python
import jax
import jax.numpy as jnp
from jax import lax
from jax.sharding import PartitionSpec as P

SPAN = 256


precise = lax.Precision.HIGHEST


def entering_2(value, axis, join, neutral):
    count, mine = (lax.axis_size(axis), lax.axis_index(axis))
    pieces = jax.tree.map(lambda part: lax.all_gather(part, axis), value)
    total = jax.tree.map(
        lambda part, zero: jnp.full_like(part, 0) + jnp.asarray(zero, part.dtype), value, neutral
    )

    def lap(position, total):
        longer = join(total, jax.tree.map(lambda part: part[position], pieces))
        return jax.tree.map(lambda new, old: jnp.where(position < mine, new, old), longer, total)

    return lax.fori_loop(0, count - 1, lap, total)


def span_basics(span_a, span_s):
    length = span_a.shape[-1]
    reset_positions = jnp.arange(length)
    triangle = (reset_positions[:, None] <= reset_positions[None, :]).astype(jnp.float32)
    cum_decay = jnp.dot(span_a.astype(jnp.float32), triangle, precision=precise)
    doc_index = jnp.dot(span_s.astype(jnp.float32), triangle, precision=precise)
    return (reset_positions, cum_decay, doc_index)


def diag_part(span_x, span_b, span_c, span_a, span_s):
    reset_positions, cum_decay, doc_index = span_basics(span_a, span_s)
    head_count = span_a.shape[0]
    length = span_x.shape[0]
    same_doc = (reset_positions[:, None] >= reset_positions[None, :]) & (
        doc_index[:, None] == doc_index[None, :]
    )
    decay_gaps = cum_decay[:, :, None] - cum_decay[:, None, :]
    decay_mat = jnp.where(same_doc, jnp.exp(jnp.minimum(decay_gaps, 0.0)), 0.0)
    scores = jnp.einsum("in,jn->ij", span_c, span_b, preferred_element_type=jnp.float32)
    weights = (decay_mat * scores[None]).astype(jnp.bfloat16)
    per_head = span_x.reshape(length, head_count, -1)
    diag_out = jnp.einsum("hij,jhp->ihp", weights, per_head, preferred_element_type=jnp.float32)
    return diag_out.astype(jnp.bfloat16).reshape(length, -1)


def state_part(span_x, span_b, span_a, span_s):
    reset_positions, cum_decay, doc_index = span_basics(span_a, span_s)
    head_count = span_a.shape[0]
    length = span_x.shape[0]
    last_cum = cum_decay[:, -1]
    end_keep = jnp.where(
        doc_index[None, :] == doc_index[-1], jnp.exp(last_cum[:, None] - cum_decay), 0.0
    )
    weighted_b = (end_keep[:, :, None] * span_b[None].astype(jnp.float32)).astype(jnp.bfloat16)
    per_head = span_x.reshape(length, head_count, -1)
    span_state = jnp.einsum(
        "hjn,jhp->hpn", weighted_b, per_head, preferred_element_type=jnp.float32
    )
    span_total = jnp.where(doc_index[-1] == 0, jnp.exp(last_cum), 0.0)
    entry_keep = jnp.where(doc_index[None, :] == 0, jnp.exp(cum_decay), 0.0)
    return (span_state, span_total, entry_keep)


def combine_carry(earlier, later):
    return (earlier[0] * later[0], later[0][:, None, None] * earlier[1] + later[1])


def local_diag(span_items):
    return lax.map(lambda one_span: diag_part(*one_span), span_items)


def pass_carry(device_pair, start_pair):
    return entering_2(device_pair, "ctx", combine_carry, start_pair)[1]


def within_outputs(x_blocks, b_blocks, c_blocks, a_blocks, s_blocks):
    return local_diag((x_blocks, b_blocks, c_blocks, a_blocks, s_blocks))


def body(inputs, b_proj, c_proj, log_decay, starts, counts, skip_gain, readout):
    tokens = inputs.shape[1]
    length = SPAN
    blocks = tokens // length
    head_count = log_decay.shape[1]
    live_count = counts[0, 0]
    live_mask = jnp.arange(tokens) < live_count
    masked_x = jnp.where(live_mask[:, None], inputs[0], jnp.zeros((), inputs.dtype))
    masked_a = jnp.where(live_mask[None, :], log_decay[0], jnp.zeros((), log_decay.dtype))
    masked_s = jnp.where(live_mask, starts[0], 0)
    x_blocks = masked_x.reshape(blocks, length, -1)
    b_blocks = b_proj[0].reshape(blocks, length, -1)
    c_blocks = c_proj[0].reshape(blocks, length, -1)
    a_blocks = masked_a.reshape(head_count, blocks, length).transpose(1, 0, 2)
    s_blocks = masked_s.reshape(blocks, length)
    state_all, total_all, entry_all = lax.map(
        lambda one_span: state_part(*one_span), (x_blocks, b_blocks, a_blocks, s_blocks)
    )

    def fold_span(carried, span_items):
        total_now, state_now = span_items
        return ((carried[0] * total_now, total_now[:, None, None] * carried[1] + state_now), None)

    start_pair = (jnp.ones((head_count,), jnp.float32), jnp.zeros(state_all.shape[1:], jnp.float32))
    device_pair, unused_out = lax.scan(fold_span, start_pair, (total_all, state_all))
    diag_all = within_outputs(x_blocks, b_blocks, c_blocks, a_blocks, s_blocks)
    diag_all, device_pair = lax.optimization_barrier((diag_all, device_pair))
    carried_in = pass_carry(device_pair, start_pair)

    def enter_span(carried, span_items):
        total_now, state_now = span_items
        return (total_now[:, None, None] * carried + state_now, carried)

    final_state, entering = lax.scan(enter_span, carried_in, (total_all, state_all))
    off_out = jnp.einsum(
        "kin,khpn->kihp",
        c_blocks,
        entering.astype(jnp.bfloat16),
        preferred_element_type=jnp.float32,
    )
    per_head = x_blocks.reshape(blocks, length, head_count, -1)
    mixed_out = diag_all.reshape(blocks, length, head_count, -1).astype(jnp.float32)
    mixed_out = mixed_out + off_out * jnp.transpose(entry_all, (0, 2, 1))[..., None]
    mixed_out = mixed_out + skip_gain[None, None, :, None] * per_head.astype(jnp.float32)
    live_rows = live_mask.reshape(blocks, length).astype(jnp.float32)
    mixed_out = (mixed_out * live_rows[:, :, None, None]).astype(jnp.bfloat16)
    ssd_out = mixed_out.reshape(1, tokens, -1)
    token_part = jnp.dot(ssd_out[0], readout, preferred_element_type=jnp.float32)
    token_scores = lax.psum(token_part, "head")
    return (ssd_out, token_scores.reshape(1, tokens))


def solution(mesh):
    placed = (
        P("rep", "ctx", "head"),
        P("rep", "ctx", "head"),
        P("rep", "ctx", "head"),
        P("rep", "head", "ctx"),
        P("rep", "ctx"),
        P("rep", "ctx"),
        P("head"),
        P("head"),
    )
    return jax.shard_map(
        body,
        mesh=mesh,
        in_specs=placed,
        out_specs=(P("rep", "ctx", "head"), P("rep", "ctx")),
        check_vma=False,
    )
```

profile of v0, /device:TPU:4, one launch (start us, length us, event | category | flops | bytes accessed | tf_op | source)
XLA Modules:
  0.0 198.0 jit_solution(17420713588232635263)
XLA Ops:
  9.7 2.4 %broadcast_select_fusion.1 = bf16[2,256,1024]{2,1,0:T(8,128)(2,1)} fusion(bf16[2,256,1024]{2,1,0:T(8,128)(2,1)} %bitcast.168, pred[2,256]{1,0:T(4,128)(4,1)S(1)} %get-tuple-element.384), kind=kLoop, calls=%fused_computation.69 | loop fusion | flops 524288 | bytes 2097664 | tf_op jit(solution)/shard_map/jit(_where)/select_n | solution.py:92
  12.2 2.3 %copy.21 = bf16[2,256,1024]{1,2,0:T(8,128)(2,1)} copy(bf16[2,256,1024]{2,1,0:T(8,128)(2,1)} %broadcast_select_fusion.1) | data formatting | bytes 2097152 | tf_op jit(solution)/shard_map/while | solution.py:74
  14.5 9.0 %while.69 = (s32[]{:T(128)}, f32[2,16,64,256]{3,2,1,0:T(8,128)S(1)}, f32[2,16]{1,0:T(2,128)S(1)}, f32[2,16,256]{2,1,0:T(8,128)S(1)}, bf16[2,256,1024]{1,2,0:T(8,...) while((s32[]{:T(128)}, ...), condition=%wide.region_3.4_spmd.clone, body=%wide.region_2.3_spmd.sunk.clone | while | flops 139408144 | bytes 3372799 | solution.py:100
  25.0 10.6 %while.68 = (s32[]{:T(128)}, bf16[2,256,1024]{1,2,0:T(8,128)(2,1)}, bf16[2,256,1024]{1,2,0:T(8,128)(2,1)}, s32[2,256]{1,0:T(2,128)S(1)}, bf16[2,16,256]{2,1,0:T(...) while((s32[]{:T(128)}, bf16[2,256,1024]{1,2,0:T(8,128)(2,1)}, ...), condition=%wide.region_1.2_spmd.clone, body=%wide.region_0.1_spmd.sunk.clone | while | flops 176488704 | bytes 12497045 | solution.py:74
  27.7 1.6 fusion.95
  32.9 1.6 fusion.95
  35.6 4.0 %reshape.119 = bf16[2,256,16,64]{3,2,1,0:T(8,128)(2,1)} reshape(bf16[1,512,1024]{2,1,0:T(8,128)(2,1)} %param.18) | data formatting | bytes 2097152 | tf_op jit(solution)/shard_map/squeeze | solution.py:92
  41.8 34.5 %all-reduce = f32[256]{0:T(256)S(1)} all-reduce(f32[256]{0:T(256)S(1)} %dynamic-update-slice), channel_id=2, replica_groups=mesh['head'=8,'ctx'=16,'rep'=4] {'ctx'}, use_global_device_ids=true, to_apply=%add | all-reduce | flops 256 | bytes 2048
  76.3 3.7 %copy.26 = bf16[2,256,16,64]{1,3,2,0:T(8,128)(2,1)} copy(bf16[2,256,16,64]{3,2,1,0:T(8,128)(2,1)} %reshape.119) | data formatting | bytes 2097152 | tf_op jit(solution)/shard_map/squeeze | solution.py:92
  81.1 58.3 %all-gather.4.cloned.1.call-done = f32[256,64,256]{2,1,0:T(8,128)} async-done(((f32[16,64,256]{2,1,0:T(8,128)}), f32[256,64,256]{2,1,0:T(8,128)}) %all-gather.4.cloned.1.call-update) | async-done | bytes 16777232 | tf_op jit(solution)/shard_map/all_gather | solution.py:14
  139.4 22.5 %while.72 = (s32[]{:T(128)}, f32[16,64,256]{2,1,0:T(8,128)S(1)}, s32[]{:T(128)}, f32[16,16]{1,0:T(8,128)S(1)}, f32[16,16,64,256]{3,2,1,0:T(8,128)}) while((s32[]{:T(128)}, f32[16,64,256]{2,1,0:T(8,128)S(1)}, s32[]{:T(128)}, f32[16,16]{1,0:T(8,128)S(1)}, f32[16,16,64,256]{3,2,1,0:T(8,128)}) %tuple.153), condition=%wide.region_7.8_spmd.clone.clone, body=%wide.region_6.7_spmd.clone.sunk.clone | while | flops 1048580 | bytes 3146009 | solution.py:23
  140.9 1.5 fusion.102
  142.4 1.5 fusion.102
  143.9 1.5 fusion.102
  145.4 1.5 fusion.102
  146.9 1.5 fusion.102
  148.4 1.5 fusion.102
  149.9 1.5 fusion.102
  161.9 2.3 %while.70 = (s32[]{:T(128)}, f32[16,64,256]{2,1,0:T(8,128)S(1)}, bf16[2,16,64,256]{3,2,1,0:T(8,128)(2,1)}, f32[2,16]{1,0:T(2,128)S(1)}, f32[2,16,64,256]{3,2,1,0:T(8,128)S(1)}) while((s32[]{:T(128)}, f32[16,64,256]{2,1,0:T(8,128)S(1)}, bf16[2,16,64,256]{3,2,1,0:T(8,128)(2,1)}, f32[2,16]{1,0:T(2,128)S(1)}, ...), condition=%wide.region_9.10_spmd.clone, body=%wide.region_8.9_spmd.sunk.clone | while | flops 524290 | bytes 5243653 | solution.py:118
  164.2 2.6 %fusion.41 = bf16[2,256,16,64]{1,3,2,0:T(8,128)(2,1)S(1)} fusion(bf16[2,256,16,64]{1,3,2,0:T(8,128)(2,1)} %bitcast.178, bf16[2,256,256,1]{2,1,3,0:T(8,128)(2,1)S(1)} %bitcast.173, f32[2,256]{1,0:T(2,128)S(1)} %get-tuple-element.385, bf16[2,256,16,64]{1,3,2,0:T(8,128)(2,1)} %copy.26, f32[16]{0:T(128)S(1)} %copy-done.8, f32[2,256,16]{1,2,0:T(8,128)S(1)} %bitcast.179, ...), kind=kOutput, calls=%fused_computation.66 | convolution fusion | flops 273154048 | bytes 4491840 | tf_op jit(solution)/shard_map/kin,khpn->kihp/dot_general | solution.py:119
  166.8 2.0 %copy.33 = bf16[2,256,16,64]{3,2,1,0:T(8,128)(2,1)S(1)} copy(bf16[2,256,16,64]{1,3,2,0:T(8,128)(2,1)S(1)} %fusion.41) | data formatting | bytes 2097152
  168.8 2.1 %copy.27 = bf16[2,256,16,64]{1,0,3,2:T(2,128)(2,1)} copy(bf16[2,256,16,64]{1,3,2,0:T(8,128)(2,1)S(1)} %fusion.41) | data formatting | bytes 2097152 | tf_op jit(solution)/shard_map/convert_element_type | solution.py:130
  170.8 2.3 %reshape.120 = bf16[1,512,1024]{2,1,0:T(8,128)(2,1)} reshape(bf16[2,256,16,64]{3,2,1,0:T(8,128)(2,1)S(1)} %copy.33) | data formatting | bytes 2097152
  173.6 17.5 %psum.7 = f32[1,512]{1,0:T(1,128)} all-reduce(f32[1,512]{1,0:T(1,128)S(1)} %fusion.45), channel_id=1, replica_groups=mesh['head'=8,'ctx'=16,'rep'=4] {'head'}, use_global_device_ids=true, to_apply=%region_10.11 | all-reduce | flops 512 | bytes 4096 | tf_op jit(solution)/shard_map/psum | solution.py:133
  (113 shorter events, 36.0 us)
Async XLA Ops:
  7.2 132.2 %all-gather.4.cloned.1.call-start = ((), (), s32[]{:S(2)}) async-start(), calls=%async_computation | async-start | bytes 17825792 | tf_op jit(solution)/shard_map/all_gather | solution.py:14
  9.7 4.7 %copy-start.4 = (bf16[1,16,512]{2,1,0:T(8,128)(2,1)S(1)}, bf16[1,16,512]{2,1,0:T(8,128)(2,1)}, u32[]{:S(2)}) copy-start(bf16[1,16,512]{2,1,0:T(8,128)(2,1)} %param.21) | copy-start | bytes 49156
  9.7 4.8 %copy-start.1 = (bf16[1,512,256]{2,1,0:T(8,128)(2,1)S(1)}, bf16[1,512,256]{2,1,0:T(8,128)(2,1)}, u32[]{:S(2)}) copy-start(bf16[1,512,256]{2,1,0:T(8,128)(2,1)} %param.19) | copy-start | bytes 786436
  24.0 1.0 copy-start
  27.7 1.6 copy-start.6
  29.3 1.0 copy-start.7
  32.9 1.6 copy-start.6
  34.6 1.0 copy-start.7
  39.6 40.4 %copy-start.5 = (bf16[1024]{0:T(1024)(128)(2,1)S(1)}, bf16[1024]{0:T(1024)(128)(2,1)}, u32[]{:S(2)}) copy-start(bf16[1024]{0:T(1024)(128)(2,1)} %param.25) | copy-start | bytes 6148
  161.9 2.3 %copy-start.3 = (bf16[2,256,256]{2,1,0:T(8,128)(2,1)S(1)}, bf16[2,256,256]{2,1,0:T(8,128)(2,1)}, u32[]{:S(2)}) copy-start(bf16[2,256,256]{2,1,0:T(8,128)(2,1)} %get-tuple-element.766) | copy-start | bytes 786436
  161.9 2.3 %copy-start.8 = (f32[16]{0:T(128)S(1)}, f32[16]{0:T(128)}, u32[]{:S(2)}) copy-start(f32[16]{0:T(128)} %param.24) | copy-start | bytes 196
  170.8 2.3 %copy-start.2 = (bf16[2,256,16,64]{1,0,3,2:T(2,128)(2,1)S(1)}, bf16[2,256,16,64]{1,0,3,2:T(2,128)(2,1)}, u32[]{:S(2)}) copy-start(bf16[2,256,16,64]{1,0,3,2:T(2,128)(2,1)} %copy.27) | copy-start | bytes 3145732
Sparse Core Ops, SparseCore 0:
  35.7 103.6 all-gather.3
where the time goes:
time: 199 us; the launch traced here: 198 us
  waiting for transfers between devices  58.3 us (29%)
  blocking collectives  52 us (26%)
  other arithmetic  29.8 us (15%)
  local copies, waits for them, and re-layouts  29.4 us (15%)
  between operations  15.5 us (8%)
  matrix products  11 us (6%)
    all_gather x1, waiting for transfers between devices, entering_2(): pieces = jax.tree.map(lambda part: lax.all_gather(part, axis), value)  58.3 us
    unnamed x1, blocking collectives  34.5 us
    select_n x15, other arithmetic, lap(): jnp.where(position < mine, new, old)  21.9 us
    psum x1, blocking collectives, body(): token_scores = lax.psum(token_part, 'head')  17.5 us
    squeeze x2, local copies, waits for them, and re-layouts, body(): inputs[0]  7.72 us
    unnamed x22, local copies, waits for them, and re-layouts  7.55 us
    dynamic_slice x4, local copies, waits for them, and re-layouts, body(): lax.map(lambda one_span: state_part(*one_span), (x_blocks, b_blocks, a_bl...  4.33 us
  transfers between devices with their start and end apart: 1, of which 1 were waited for; matrix products, arithmetic and copies ran while one was open for 5% of the time, Pallas kernels for 0%

commit v1 on v0

v1 whole, which is shorter than its diff:
```python
import functools
import math

import jax
import jax.numpy as jnp
from jax import lax
from jax.experimental import pallas as pl
from jax.experimental.pallas import tpu as pltpu
from jax.sharding import PartitionSpec as P

SPAN = 256
HALF = 128
SUB = 64
LANES = 128
ROWS_STEP = 128
LOG2E = math.log2(math.e)
F32 = jnp.float32
BF16 = jnp.bfloat16
MESH = pl.DeviceIdType.MESH


def mm(a, b):
    return lax.dot_general(a, b, (((1,), (0,)), ((), ())), preferred_element_type=F32)


def mm_nt(a, b):
    return lax.dot_general(a, b, (((1,), (1,)), ((), ())), preferred_element_type=F32)


def mm_tn(a, b):
    return lax.dot_general(a, b, (((0,), (0,)), ((), ())), preferred_element_type=F32)


def iota(shape, dim):
    return lax.broadcasted_iota(jnp.int32, shape, dim)


def kernel(
    sizes,
    count_ref, x_ref, b_ref, c_ref, a_ref, s_ref, gain_ref, read_ref,
    out_ref, score_ref,
    xm, lx, cum, doc, bt, first, whole, ta, td, sbf, srecv, trecv,
    comb, tcomb, base, tbase, ein, snd, eown, psnd, y, gb, gm, sums,
    psem_s, psem_r, tsem, csem_s, csem_r, fsem_s, fsem_r, ysem_s, ysem_r,
):
    ctxs, heads_axis, tokens, tiles = sizes
    half = tiles // 2
    spans = tokens // SPAN
    steps = SPAN // ROWS_STEP
    last_chip = ctxs // 2 - 1
    ctx = lax.axis_index("ctx")
    core = lax.rem(ctx, 2)
    chip = ctx // 2
    mine = lax.axis_index("head")
    partner = ctx + 1 - 2 * core
    follow = lax.rem(ctx + 2, ctxs)
    before = lax.rem(ctx + ctxs - 2, ctxs)

    barrier = pltpu.get_barrier_semaphore()
    for other in (partner, follow, before):
        pl.semaphore_signal(barrier, inc=1, device_id={"ctx": other}, device_id_type=MESH)
    for k in range(1, heads_axis):
        pl.semaphore_signal(
            barrier, inc=1, device_id={"head": lax.rem(mine + k, heads_axis)}, device_id_type=MESH
        )

    count = count_ref[0, 0]
    live_row = iota((1, tokens), 1) < count
    log_decay = jnp.where(live_row, a_ref[0].astype(F32), 0.0).astype(BF16)
    starts = jnp.where(live_row, s_ref[...].astype(F32), 0.0)
    head_rows = log_decay.shape[0]
    starts = jnp.where(iota((head_rows, tokens), 0) == 0, starts, 0.0).astype(BF16)
    spread = (iota((head_rows, tiles * LANES), 0) == iota((head_rows, tiles * LANES), 1) // SUB)
    spread = jnp.where(spread, 1.0, 0.0).astype(BF16)
    ones = jnp.ones((head_rows, LANES), BF16)
    tri = jnp.where(iota((SPAN, SPAN), 0) >= iota((SPAN, SPAN), 1), 1.0, 0.0).astype(BF16)
    for s in range(spans):
        rows = pl.ds(s * SPAN, SPAN)
        lx[rows, :] = mm_tn(log_decay[:, s * SPAN : (s + 1) * SPAN], spread).astype(BF16)
        spread_starts = mm_tn(starts[:, s * SPAN : (s + 1) * SPAN], ones).astype(BF16)
        doc[rows, :] = mm(tri, spread_starts)
        bt[:, rows] = b_ref[0, rows, :].astype(F32).T.astype(BF16)

    live = iota((tokens, LANES), 0) < count

    def state_tile(t):
        cols = pl.ds(pl.multiple_of(t * LANES, LANES), LANES)
        xt = jnp.where(live, x_ref[0, :, cols].astype(F32), 0.0).astype(BF16)
        xm[t] = xt
        states, totals = [], []
        for s in range(spans):
            rows = slice(s * SPAN, (s + 1) * SPAN)
            run = mm(tri, lx[pl.ds(s * SPAN, SPAN), cols]) * LOG2E
            cum[t, pl.ds(s * SPAN, SPAN), :] = run
            docs = doc[pl.ds(s * SPAN, SPAN), :]
            last = run[SPAN - 1 : SPAN, :]
            keep = jnp.where(docs == docs[SPAN - 1 : SPAN, :], jnp.exp2(last - run), 0.0)
            weighted = (xt[rows, :].astype(F32) * keep).astype(BF16)
            states.append(mm(bt[:, pl.ds(s * SPAN, SPAN)], weighted))
            totals.append(jnp.where(docs[SPAN - 1 : SPAN, :] == 0.0, jnp.exp2(last), 0.0))
        first[t] = states[0]
        joined = totals[1] * states[0] + states[1]
        whole[t] = joined
        ta[t] = jnp.broadcast_to(totals[0], (8, LANES))
        td[t] = jnp.broadcast_to(totals[0] * totals[1], (8, LANES))
        return joined

    for j in range(half):
        sbf[j] = state_tile((1 - core) * half + j).astype(BF16)
        if j == 0:
            pl.semaphore_wait(barrier, 3 + heads_axis - 1)
        state_copy(sbf, srecv, psem_s, psem_r, j, partner).start()
    t_copy = pltpu.make_async_remote_copy(
        src_ref=td.at[pl.ds((1 - core) * half, half)],
        dst_ref=trecv,
        send_sem=tsem.at[0],
        recv_sem=tsem.at[1],
        device_id={"ctx": partner},
        device_id_type=MESH,
    )
    t_copy.start()
    for j in range(half):
        state_tile(core * half + j)

    t_copy.wait_recv()
    for j in range(half):
        state_copy(sbf, srecv, psem_s, psem_r, j, partner).wait_recv()
        own, theirs = whole[core * half + j], srecv[j].astype(F32)
        t_own, t_theirs = td[core * half + j], trecv[j]
        is_low = core == 0
        low, high = jnp.where(is_low, own, theirs), jnp.where(is_low, theirs, own)
        t_low, t_high = jnp.where(is_low, t_own, t_theirs), jnp.where(is_low, t_theirs, t_own)
        comb[j] = t_high[0:1, :] * low + high
        tcomb[j] = t_high * t_low
        base[j] = low
        tbase[j] = t_low

    def chain_copy(j, r):
        piece = pl.ds(r * ROWS_STEP, ROWS_STEP)
        return pltpu.make_async_remote_copy(
            src_ref=snd.at[j, piece],
            dst_ref=ein.at[j, piece],
            send_sem=csem_s.at[j, r],
            recv_sem=csem_r.at[j, r],
            device_id={"ctx": follow},
            device_id_type=MESH,
        )

    def pass_copy(j, r):
        piece = pl.ds(r * ROWS_STEP, ROWS_STEP)
        return pltpu.make_async_remote_copy(
            src_ref=psnd.at[j, piece],
            dst_ref=eown.at[core * half + j, piece],
            send_sem=fsem_s.at[j, r],
            recv_sem=fsem_r.at[j, r],
            device_id={"ctx": partner},
            device_id_type=MESH,
        )

    def local_part():
        for s in range(spans):
            rows = pl.ds(s * SPAN, SPAN)
            scores = mm_nt(c_ref[0, rows, :], b_ref[0, rows, :])
            gb[s] = scores.astype(BF16)
        lane = iota((SUB, LANES), 1)
        lane = jnp.where(lane < SUB, lane, lane - SUB)
        row = iota((SUB, LANES), 0)
        eye = jnp.where(row == lane, 1.0, 0.0)
        for k in range(tokens // SUB):
            rows = pl.ds(k * SUB, SUB)
            bk = b_ref[0, rows, :]
            sc = mm_nt(c_ref[0, rows, :], jnp.concatenate([bk, bk], axis=0))
            dk = doc[rows, :]
            drow = jnp.sum(dk * eye, axis=0, keepdims=True)
            gm[k] = jnp.where((row >= lane) & (dk == drow), sc, 0.0)
        low_lane = iota((SUB, LANES), 1) < SUB
        one_lane = iota((1, LANES), 1) < SUB

        def tile(t, _):
            skip = jnp.where(one_lane, gain_ref[2 * t], gain_ref[2 * t + 1])
            for s in range(spans):
                o = s * SPAN

                def level(at, width):
                    lo, hi = pl.ds(o + at, width), pl.ds(o + at + width, width)
                    run_lo, run_hi = cum[t, lo, :], cum[t, hi, :]
                    doc_lo, doc_hi = doc[lo, :], doc[hi, :]
                    ref, ref_doc = run_lo[width - 1 : width, :], doc_lo[width - 1 : width, :]
                    keep = jnp.where(doc_lo == ref_doc, jnp.exp2(ref - run_lo), 0.0)
                    enter = jnp.where(doc_hi == ref_doc, jnp.exp2(run_hi - ref), 0.0)
                    weighted = (xm[t, lo, :].astype(F32) * keep).astype(BF16)
                    part = gb[s, at + width : at + 2 * width, at : at + width]
                    return enter * mm(part, weighted)

                far = level(0, HALF)
                near = [level(0, SUB), level(HALF, SUB)]
                for q in range(SPAN // SUB):
                    rows = pl.ds(o + q * SUB, SUB)
                    run = cum[t, rows, :]
                    xq = xm[t, rows, :]
                    xf = xq.astype(F32)
                    run_row = jnp.sum(run * eye, axis=0, keepdims=True)
                    w = jnp.exp2(jnp.minimum(run - run_row, 0.0)) * gm[s * (SPAN // SUB) + q]
                    left = jnp.where(low_lane, xf, 0.0).astype(BF16)
                    right = jnp.where(low_lane, 0.0, xf).astype(BF16)
                    v = mm(w.astype(BF16), jnp.concatenate([left, right], axis=0))
                    v = v + skip * xf
                    if q % 2 == 1:
                        v = v + near[q // 2]
                    if q >= 2:
                        v = v + far[(q - 2) * SUB : (q - 1) * SUB, :]
                    y[t, rows, :] = v
            return 0

        lax.fori_loop(0, tiles, tile, 0)

    early = chip < (last_chip + 1) // 2
    pl.when(jnp.logical_not(early))(local_part)

    @pl.when(chip == 0)
    def _():
        ein[...] = jnp.zeros_like(ein)

    for j in range(half):
        for r in range(steps):
            piece = pl.ds(r * ROWS_STEP, ROWS_STEP)
            pl.when(chip > 0)(lambda: chain_copy(j, r).wait_recv())
            e16 = ein[j, piece, :]
            e = e16.astype(F32)

            @pl.when(chip < last_chip)
            def _():
                snd[j, piece, :] = (tcomb[j, 0:1, :] * e + comb[j, piece, :]).astype(BF16)
                chain_copy(j, r).start()

            f = tbase[j, 0:1, :] * e + base[j, piece, :]
            eown[core * half + j, piece, :] = jnp.where(core == 0, e, f).astype(BF16)
            psnd[j, piece, :] = jnp.where(core == 0, f, e).astype(BF16)
            pass_copy(j, r).start()

    pl.when(early)(local_part)

    row_scores = jnp.zeros((8, tokens), F32)

    def finish_tile(t, row_scores):
        cols = pl.ds(pl.multiple_of(t * LANES, LANES), LANES)
        e0 = eown[t]
        e1 = (ta[t][0:1, :] * e0.astype(F32) + first[t]).astype(BF16)
        parts = []
        for s, e in enumerate((e0, e1)):
            rows = pl.ds(s * SPAN, SPAN)
            enter = jnp.where(doc[rows, :] == 0.0, jnp.exp2(cum[t, rows, :]), 0.0)
            v = y[t, rows, :] + enter * mm(c_ref[0, rows, :], e)
            v = jnp.where(live[s * SPAN : (s + 1) * SPAN, :], v, 0.0).astype(BF16)
            out_ref[0, rows, cols] = v
            parts.append(v)
        v = jnp.concatenate(parts, axis=0)
        weight = jnp.broadcast_to(read_ref[:, cols].astype(F32), (16, LANES)).astype(BF16)
        return row_scores + mm_nt(weight, v)[0:8, :]

    for j in range(half):
        row_scores = finish_tile(core * half + j, row_scores)
    for j in range(half):
        for r in range(steps):
            piece = pl.ds(r * ROWS_STEP, ROWS_STEP)
            pltpu.make_async_remote_copy(
                src_ref=psnd.at[j, piece],
                dst_ref=eown.at[(1 - core) * half + j, piece],
                send_sem=fsem_s.at[j, r],
                recv_sem=fsem_r.at[j, r],
                device_id={"ctx": partner},
                device_id_type=MESH,
            ).wait_recv()
        row_scores = finish_tile((1 - core) * half + j, row_scores)

    for i in range(tokens // LANES):
        sums[mine, i : i + 1, :] = row_scores[0:1, i * LANES : (i + 1) * LANES]

    def score_copy(k):
        return pltpu.make_async_remote_copy(
            src_ref=sums.at[mine],
            dst_ref=sums.at[mine],
            send_sem=ysem_s.at[k],
            recv_sem=ysem_r.at[k],
            device_id={"head": lax.rem(mine + k, heads_axis)},
            device_id_type=MESH,
        )

    for k in range(1, heads_axis):
        score_copy(k).start()
    for k in range(1, heads_axis):
        score_copy(k).wait()
    total = sums[0]
    for k in range(1, heads_axis):
        total = total + sums[k]
    for i in range(tokens // LANES):
        score_ref[:, i * LANES : (i + 1) * LANES] = total[i : i + 1, :]

    for j in range(half):
        state_copy(sbf, srecv, psem_s, psem_r, j, partner).wait_send()
        for r in range(steps):
            pass_copy(j, r).wait_send()

            @pl.when(chip < last_chip)
            def _():
                chain_copy(j, r).wait_send()
    t_copy.wait_send()


def state_copy(src, dst, send, recv, j, partner):
    return pltpu.make_async_remote_copy(
        src_ref=src.at[j],
        dst_ref=dst.at[j],
        send_sem=send.at[j],
        recv_sem=recv.at[j],
        device_id={"ctx": partner},
        device_id_type=MESH,
    )


def body(inputs, b_proj, c_proj, log_decay, starts, counts, skip_gain, readout):
    tokens, width = inputs.shape[1:]
    ctxs, heads_axis = lax.axis_size("ctx"), lax.axis_size("head")
    tiles = width // LANES
    half = tiles // 2
    spans = tokens // SPAN
    steps = SPAN // ROWS_STEP
    vmem, smem = pl.BlockSpec(memory_space=pltpu.VMEM), pl.BlockSpec(memory_space=pltpu.SMEM)
    big = lambda n, dtype: pltpu.VMEM((n, SPAN, LANES), dtype)
    small = lambda n: pltpu.VMEM((n, 8, LANES), F32)
    sem = pltpu.SemaphoreType.DMA
    return pl.pallas_call(
        functools.partial(kernel, (ctxs, heads_axis, tokens, tiles)),
        out_shape=(
            jax.ShapeDtypeStruct(inputs.shape, BF16),
            jax.ShapeDtypeStruct((1, tokens), F32),
        ),
        in_specs=[smem, vmem, vmem, vmem, vmem, vmem, smem, vmem],
        out_specs=(vmem, vmem),
        scratch_shapes=[
            pltpu.VMEM((tiles, tokens, LANES), BF16),
            pltpu.VMEM((tokens, width), BF16),
            pltpu.VMEM((tiles, tokens, LANES), F32),
            pltpu.VMEM((tokens, LANES), F32),
            pltpu.VMEM((SPAN, tokens), BF16),
            big(tiles, F32),
            big(tiles, F32),
            small(tiles),
            small(tiles),
            big(half, BF16),
            big(half, BF16),
            small(half),
            big(half, F32),
            small(half),
            big(half, F32),
            small(half),
            big(half, BF16),
            big(half, BF16),
            big(tiles, BF16),
            big(half, BF16),
            pltpu.VMEM((tiles, tokens, LANES), F32),
            pltpu.VMEM((spans, SPAN, SPAN), BF16),
            pltpu.VMEM((tokens // SUB, SUB, LANES), F32),
            pltpu.VMEM((heads_axis, tokens // LANES, LANES), F32),
            sem((half,)), sem((half,)), sem((2,)),
            sem((half, steps)), sem((half, steps)),
            sem((half, steps)), sem((half, steps)),
            sem((heads_axis,)), sem((heads_axis,)),
        ],
        compiler_params=pltpu.CompilerParams(collective_id=0, has_side_effects=True),
        name="ssd",
    )(counts, inputs, b_proj, c_proj, log_decay, starts, skip_gain, readout.reshape(1, width))


def solution(mesh):
    placed = (
        P("rep", "ctx", "head"),
        P("rep", "ctx", "head"),
        P("rep", "ctx", "head"),
        P("rep", "head", "ctx"),
        P("rep", "ctx"),
        P("rep", "ctx"),
        P("head"),
        P("head"),
    )
    return jax.shard_map(
        body,
        mesh=mesh,
        in_specs=placed,
        out_specs=(P("rep", "ctx", "head"), P("rep", "ctx")),
        check_vma=False,
    )
```

time: 199 us -> 48.8 us (0.25)
  the two profiles are of different devices: /device:TPU:4 before, /device:TPU:448 now
where the time goes in v1:
time: 48.8 us; the launch traced here: 48.6 us
  Pallas kernels  43.2 us (89%)
  local copies, waits for them, and re-layouts  4.12 us (8%)
  between operations  1.29 us (3%)
    pallas_call x1, Pallas kernels, body(): pl.pallas_call(functools.partial(kernel, (ctxs, heads_axis, tokens, tiles...  43.2 us
    unnamed x4, local copies, waits for them, and re-layouts  2.85 us
    reshape x1, local copies, waits for them, and re-layouts, body(): readout.reshape(1, width)  1.28 us

profile of v1, /device:TPU:448, one launch (start us, length us, event | category | flops | bytes accessed | tf_op | source)
XLA Modules:
  0.0 48.6 jit_solution(12793657985095350184)
XLA Ops:
  1.3 1.3 %reshape.7.read_ref = bf16[1,1024]{1,0:T(2,128)(2,1)} reshape(bf16[1024]{0:T(1024)(128)(2,1)} %param.15) | data formatting | bytes 4096 | tf_op jit(solution)/shard_map/reshape | solution.py:372
  2.6 43.2 %ssd.1 = (bf16[1,512,1024]{2,1,0:T(8,128)(2,1)}, f32[1,512]{1,0:T(1,128)}) custom-call(s32[1,1]{1,0:T(1,128)S(6)} %copy.12.count_ref, bf16[1,512,1024]{2,1,0:T(8,128)(2,1)} %x_ref.1, bf16[1,512,256]{2,1,0:T(8,128)(2,1)} %b_ref.1, bf16[1,512,256]{2,1,0:T(8,128)(2,1)} %c_ref.1, bf16[1,16,512]{2,1,0:T(8,128)(2,1)} %a_ref.1, s32[1,512]{1,0:T(1,128)} %s_ref.1, ...), custom_call_target="tpu_custom_call" | custom-call | tf_op jit(solution)/shard_map/ssd/pallas_call | solution.py:332
  45.8 0.0 copy-start
  45.8 2.3 %copy.13 = bf16[1,512,1024]{2,1,0:T(8,128)(2,1)} copy(bf16[1,512,1024]{2,1,0:T(8,128)(2,1)} %get-tuple-element.4) | data formatting | bytes 2097152
  48.1 0.0 copy-done
  48.1 0.6 %copy.14 = f32[1,512]{1,0:T(1,128)} copy(f32[1,512]{1,0:T(1,128)S(1)} %copy-done) | data formatting | bytes 4096
Async XLA Ops:
  45.8 2.3 %copy-start = (f32[1,512]{1,0:T(1,128)S(1)}, f32[1,512]{1,0:T(1,128)}, u32[]{:S(2)}) copy-start(f32[1,512]{1,0:T(1,128)} %get-tuple-element.5) | copy-start | bytes 6148

commit v2 on v1

--- a/solution.py
+++ b/solution.py
@@ -12,7 +12,9 @@
 HALF = 128
 SUB = 64
 LANES = 128
-ROWS_STEP = 128
+ROWS_STEP = 64
+SCORES_AT = 6
+EDGES = ((0, 1), (1, 2), (2, 3), (1, 3), (1, 7), (3, 4), (4, 5), (5, 6), (6, 7))
 LOG2E = math.log2(math.e)
 F32 = jnp.float32
 BF16 = jnp.bfloat16
@@ -39,26 +41,33 @@
     sizes,
     count_ref, x_ref, b_ref, c_ref, a_ref, s_ref, gain_ref, read_ref,
     out_ref, score_ref,
-    xm, lx, cum, doc, bt, first, whole, ta, td, sbf, srecv, trecv,
-    comb, tcomb, base, tbase, ein, snd, eown, psnd, y, gb, gm, sums,
-    psem_s, psem_r, tsem, csem_s, csem_r, fsem_s, fsem_r, ysem_s, ysem_r,
+    xm, lx, cum, doc, bt, first, whole, ta, td, sbf, srecv, mfull, msnd, mrecv,
+    comb, base, mown, mbase, inb, tin, outb, tout, eown, psnd, vent, vsnd, y, gb, gm, sums, rd,
+    psem_s, psem_r, tsem, csem_s, csem_r, vsem_s, vsem_r, fsem_s, fsem_r, wsem, ysem_s, ysem_r,
 ):
     ctxs, heads_axis, tokens, tiles = sizes
     half = tiles // 2
     spans = tokens // SPAN
     steps = SPAN // ROWS_STEP
-    last_chip = ctxs // 2 - 1
     ctx = lax.axis_index("ctx")
     core = lax.rem(ctx, 2)
     chip = ctx // 2
     mine = lax.axis_index("head")
     partner = ctx + 1 - 2 * core
-    follow = lax.rem(ctx + 2, ctxs)
-    before = lax.rem(ctx + ctxs - 2, ctxs)
 
     barrier = pltpu.get_barrier_semaphore()
-    for other in (partner, follow, before):
-        pl.semaphore_signal(barrier, inc=1, device_id={"ctx": other}, device_id_type=MESH)
+    pl.semaphore_signal(barrier, inc=1, device_id={"ctx": partner}, device_id_type=MESH)
+    peers = heads_axis
+    for ends in EDGES:
+        for here, there in (ends, ends[::-1]):
+            peers = peers + jnp.where(chip == here, 1, 0)
+
+            @pl.when(chip == here)
+            def _():
+                pl.semaphore_signal(
+                    barrier, inc=1, device_id={"ctx": 2 * there + core}, device_id_type=MESH
+                )
+
     for k in range(1, heads_axis):
         pl.semaphore_signal(
             barrier, inc=1, device_id={"head": lax.rem(mine + k, heads_axis)}, device_id_type=MESH
@@ -69,6 +78,7 @@
     log_decay = jnp.where(live_row, a_ref[0].astype(F32), 0.0).astype(BF16)
     starts = jnp.where(live_row, s_ref[...].astype(F32), 0.0)
     head_rows = log_decay.shape[0]
+    all_starts = jnp.broadcast_to(starts, (head_rows, tokens)).astype(BF16)
     starts = jnp.where(iota((head_rows, tokens), 0) == 0, starts, 0.0).astype(BF16)
     spread = (iota((head_rows, tiles * LANES), 0) == iota((head_rows, tiles * LANES), 1) // SUB)
     spread = jnp.where(spread, 1.0, 0.0).astype(BF16)
@@ -82,6 +92,31 @@
         bt[:, rows] = b_ref[0, rows, :].astype(F32).T.astype(BF16)
 
     live = iota((tokens, LANES), 0) < count
+
+    rd[...] = read_ref[...].astype(F32)
+    upper = jnp.where(iota((SPAN, SPAN), 0) <= iota((SPAN, SPAN), 1), 1.0, 0.0).astype(BF16)
+    head_of = iota((head_rows, LANES), 1) // SUB
+    read_rows = jnp.zeros((head_rows, tokens), F32)
+    for t in range(tiles):
+        part = jnp.where(iota((head_rows, LANES), 0) == 2 * t + head_of, rd[t : t + 1, :], 0.0)
+        read_rows = read_rows + mm_nt(part.astype(BF16), x_ref[0, :, t * LANES : (t + 1) * LANES])
+    read_rows = jnp.where(live_row, read_rows, 0.0)
+    enter_rows, read_states, row_totals = [], [], []
+    for s in range(spans):
+        lanes = slice(s * SPAN, (s + 1) * SPAN)
+        run = mm(log_decay[:, lanes], upper) * LOG2E
+        docs = mm(all_starts[:, lanes], upper)
+        enter_rows.append(jnp.where(docs == 0.0, jnp.exp2(run), 0.0))
+        ends = slice(SPAN - 1, SPAN)
+        keep = jnp.where(docs == docs[:, ends], jnp.exp2(run[:, ends] - run), 0.0)
+        read_states.append(mm((read_rows[:, lanes] * keep).astype(BF16), b_ref[0, pl.ds(s * SPAN, SPAN), :]))
+        row_totals.append(jnp.broadcast_to(enter_rows[s][:, ends], (head_rows, LANES)))
+    read_state = enter_rows[1][:, SPAN - 1 : SPAN] * read_states[0] + read_states[1]
+    for h in range(2):
+        rows = slice(h * 8, (h + 1) * 8)
+        for i in range(2):
+            mfull[h, 1 + i] = read_state[rows, i * LANES : (i + 1) * LANES]
+        mfull[h, 3] = row_totals[0][rows] * row_totals[1][rows]
 
     def state_tile(t):
         cols = pl.ds(pl.multiple_of(t * LANES, LANES), LANES)
@@ -108,46 +143,103 @@
     for j in range(half):
         sbf[j] = state_tile((1 - core) * half + j).astype(BF16)
         if j == 0:
-            pl.semaphore_wait(barrier, 3 + heads_axis - 1)
+            pl.semaphore_wait(barrier, peers)
         state_copy(sbf, srecv, psem_s, psem_r, j, partner).start()
     t_copy = pltpu.make_async_remote_copy(
-        src_ref=td.at[pl.ds((1 - core) * half, half)],
-        dst_ref=trecv,
+        src_ref=msnd,
+        dst_ref=mrecv,
         send_sem=tsem.at[0],
         recv_sem=tsem.at[1],
         device_id={"ctx": partner},
         device_id_type=MESH,
     )
+    msnd[...] = mfull[1 - core]
+    for j in range(half):
+        msnd[0, j : j + 1, :] = td[(1 - core) * half + j][0:1, :]
     t_copy.start()
     for j in range(half):
         state_tile(core * half + j)
+        mfull[core, 0, j : j + 1, :] = td[core * half + j][0:1, :]
+
+    def join(earlier, later):
+        columns = later[3]
+        return (
+            later[0] * earlier[0],
+            columns * earlier[1] + later[1],
+            columns * earlier[2] + later[2],
+            columns * earlier[3],
+        )
+
+    def put(ref, parts):
+        for i, part in enumerate(parts):
+            ref[i] = part
+
+    def pick(choose, a, b):
+        return tuple(jnp.where(choose, u, v) for u, v in zip(a, b))
+
+    def parts_of(ref):
+        return tuple(ref[i] for i in range(4))
 
     t_copy.wait_recv()
+    is_low = core == 0
+    own_parts, their_parts = parts_of(mfull.at[core]), parts_of(mrecv)
+    low_parts, high_parts = pick(is_low, own_parts, their_parts), pick(is_low, their_parts, own_parts)
+    put(mown, join(low_parts, high_parts))
+    put(mbase, low_parts)
     for j in range(half):
         state_copy(sbf, srecv, psem_s, psem_r, j, partner).wait_recv()
         own, theirs = whole[core * half + j], srecv[j].astype(F32)
-        t_own, t_theirs = td[core * half + j], trecv[j]
-        is_low = core == 0
         low, high = jnp.where(is_low, own, theirs), jnp.where(is_low, theirs, own)
-        t_low, t_high = jnp.where(is_low, t_own, t_theirs), jnp.where(is_low, t_theirs, t_own)
-        comb[j] = t_high[0:1, :] * low + high
-        tcomb[j] = t_high * t_low
+        comb[j] = high_parts[0][j : j + 1, :] * low + high
         base[j] = low
-        tbase[j] = t_low
-
-    def chain_copy(j, r):
-        piece = pl.ds(r * ROWS_STEP, ROWS_STEP)
+
+    def send(src, out, j, r, to, slot):
+        piece = rows_of(r)
         return pltpu.make_async_remote_copy(
-            src_ref=snd.at[j, piece],
-            dst_ref=ein.at[j, piece],
-            send_sem=csem_s.at[j, r],
-            recv_sem=csem_r.at[j, r],
-            device_id={"ctx": follow},
+            src_ref=src.at[j, piece],
+            dst_ref=inb.at[slot, j, piece],
+            send_sem=csem_s.at[out, j, r],
+            recv_sem=csem_r.at[slot, j, r],
+            device_id={"ctx": 2 * to + core},
             device_id_type=MESH,
         )
 
+    def send_t(out, to, slot, sem=None):
+        return pltpu.make_async_remote_copy(
+            src_ref=tout.at[out],
+            dst_ref=tin.at[slot],
+            send_sem=vsem_s.at[out if sem is None else sem],
+            recv_sem=vsem_r.at[slot],
+            device_id={"ctx": 2 * to + core},
+            device_id_type=MESH,
+        )
+
+    def pieces(step, begin=0, end=half * steps):
+        def one(q, _):
+            step(q // steps, lax.rem(q, steps))
+            return 0
+
+        lax.fori_loop(begin, end, one, 0)
+
+    def rows_of(r):
+        return pl.ds(pl.multiple_of(r * ROWS_STEP, ROWS_STEP), ROWS_STEP)
+
+    def of_chip(*values):
+        result = values[-1]
+        for i, value in enumerate(values[:-1]):
+            result = jnp.where(chip == i, value, result)
+        return result
+
+    def among(*chips):
+        return functools.reduce(jnp.logical_or, [chip == i for i in chips])
+
+    to_lead = of_chip(1, 0, 3, 2, 5, 4, 4, 4)
+    to_join = of_chip(1, 3, 1, 1, 4, 6, 7, 6)
+    join_slot = jnp.where(chip < 3, 1, 0)
+    to_last = of_chip(1, 7, 1, 4, 5, 4, 4, 6)
+
     def pass_copy(j, r):
-        piece = pl.ds(r * ROWS_STEP, ROWS_STEP)
+        piece = rows_of(r)
         return pltpu.make_async_remote_copy(
             src_ref=psnd.at[j, piece],
             dst_ref=eown.at[core * half + j, piece],
@@ -214,52 +306,197 @@
 
         lax.fori_loop(0, tiles, tile, 0)
 
-    early = chip < (last_chip + 1) // 2
-    pl.when(jnp.logical_not(early))(local_part)
+    @pl.when(among(0, 2, 3, 4))
+    def _():
+        tout[0] = mown[...]
+        send_t(0, to_lead, 0).start()
+
+        def step(j, r):
+            piece = rows_of(r)
+            outb[0, j, piece, :] = comb[j, piece, :].astype(BF16)
+            send(outb.at[0], 0, j, r, to_lead, 0).start()
+
+        pieces(step)
+
+    local_part()
+
+    @pl.when(among(1, 2, 3, 5, 6, 7))
+    def _():
+        send_t(0, to_lead, 0).wait_recv()
+
+    def row(ref, j):
+        return ref[0, pl.ds(j, 1), :]
+
+    is_later = chip == 2
+
+    @pl.when(among(1, 2, 5, 6))
+    def _():
+        got, own = parts_of(tin.at[0]), parts_of(mown)
+        put(tout.at[1], join(pick(is_later, own, got), pick(is_later, got, own)))
+        send_t(1, to_join, join_slot).start()
+
+    def join_step(j, r):
+        piece = rows_of(r)
+        send(outb.at[0], 0, j, r, to_lead, 0).wait_recv()
+        got, own = inb[0, j, piece, :].astype(F32), comb[j, piece, :]
+        scale = jnp.where(is_later, row(tin.at[0], j), row(mown, j))
+        joined = scale * jnp.where(is_later, own, got) + jnp.where(is_later, got, own)
+        outb[1, j, piece, :] = joined.astype(BF16)
+        send(outb.at[1], 1, j, r, to_join, join_slot).start()
+
+    @pl.when(among(2, 5, 6))
+    def _():
+        pieces(join_step)
+
+    def enter(j, r, e):
+        piece = rows_of(r)
+        f = row(mbase, j) * e + base[j, piece, :]
+        eown[core * half + j, piece, :] = jnp.where(is_low, e, f).astype(BF16)
+        psnd[j, piece, :] = jnp.where(is_low, f, e).astype(BF16)
+        pass_copy(j, r).start()
+
+    def pass_rows(side):
+        return pltpu.make_async_remote_copy(
+            src_ref=vsnd,
+            dst_ref=vent.at[side],
+            send_sem=wsem.at[0],
+            recv_sem=wsem.at[1],
+            device_id={"ctx": partner},
+            device_id_type=MESH,
+        )
+
+    def enter_rows_of(e):
+        for i in range(2):
+            f = mbase[3] * e[i] + mbase[1 + i]
+            vent[core, i] = jnp.where(is_low, e[i], f)
+            vsnd[i] = jnp.where(is_low, f, e[i])
+        pass_rows(core).start()
 
     @pl.when(chip == 0)
     def _():
-        ein[...] = jnp.zeros_like(ein)
-
-    for j in range(half):
-        for r in range(steps):
-            piece = pl.ds(r * ROWS_STEP, ROWS_STEP)
-            pl.when(chip > 0)(lambda: chain_copy(j, r).wait_recv())
-            e16 = ein[j, piece, :]
-            e = e16.astype(F32)
-
-            @pl.when(chip < last_chip)
-            def _():
-                snd[j, piece, :] = (tcomb[j, 0:1, :] * e + comb[j, piece, :]).astype(BF16)
-                chain_copy(j, r).start()
-
-            f = tbase[j, 0:1, :] * e + base[j, piece, :]
-            eown[core * half + j, piece, :] = jnp.where(core == 0, e, f).astype(BF16)
-            psnd[j, piece, :] = jnp.where(core == 0, f, e).astype(BF16)
-            pass_copy(j, r).start()
-
-    pl.when(early)(local_part)
-
-    row_scores = jnp.zeros((8, tokens), F32)
-
-    def finish_tile(t, row_scores):
+        enter_rows_of((jnp.zeros((8, LANES), F32),) * 2)
+        pieces(lambda j, r: enter(j, r, jnp.zeros((ROWS_STEP, LANES), F32)))
+
+    @pl.when(chip == 1)
+    def _():
+        enter_rows_of((tin[0, 1], tin[0, 2]))
+
+        def last_step(j, r):
+            piece = rows_of(r)
+            send(outb.at[1], 1, j, r, 1, 1).wait_recv()
+            got, own = inb[1, j, piece, :].astype(F32), outb[1, j, piece, :].astype(F32)
+            outb[2, j, piece, :] = (row(tin.at[1], j) * own + got).astype(BF16)
+            send(outb.at[2], 2, j, r, 7, 1).start()
+
+        def both(j, r):
+            join_step(j, r)
+            last_step(j - behind // steps, r)
+
+        behind = (half // 2) * steps
+        pieces(join_step, 0, behind)
+        send_t(1, 1, 1).wait_recv()
+        put(tout.at[2], join(parts_of(tout.at[1]), parts_of(tin.at[1])))
+        send_t(2, 7, 1).start()
+        pieces(both, behind, half * steps)
+        send_t(1, 2, 1, 3).start()
+        pieces(lambda j, r: send(outb.at[1], 3, j, r, 2, 1).start())
+        pieces(last_step, half * steps - behind, half * steps)
+        pieces(lambda j, r: enter(j, r, inb[0, j, rows_of(r), :].astype(F32)))
+
+    joins = among(3, 5, 6, 7)
+
+    def last_step(j, r):
+        piece = rows_of(r)
+        send(outb.at[2], 2, j, r, 1, 1).wait_recv()
+
+        @pl.when(among(4, 7))
+        def _():
+            send(inb.at[1], 2, j, r, to_last, 1).start()
+
+        @pl.when(among(3, 7))
+        def _():
+            send(outb.at[0], 0, j, r, to_lead, 0).wait_recv()
+
+        got = inb[1, j, piece, :].astype(F32)
+        add = jnp.where(joins, inb[0, j, piece, :].astype(F32), 0.0)
+        e = jnp.where(joins, row(tin.at[0], j), 1.0) * got + add
+
+        @pl.when(chip == 3)
+        def _():
+            outb[2, j, piece, :] = (row(mown, j) * e + comb[j, piece, :]).astype(BF16)
+            send(outb.at[2], 2, j, r, 4, 1).start()
+
+        enter(j, r, e)
+
+    @pl.when(chip >= 2)
+    def _():
+        send_t(2, 1, 1).wait_recv()
+
+        @pl.when(among(4, 7))
+        def _():
+            tout[2] = tin[1]
+            send_t(2, to_last, 1).start()
+
+        e = parts_of(tin.at[1])
+        e = pick(joins, join(e, parts_of(tin.at[0])), e)
+
+        @pl.when(chip == 3)
+        def _():
+            put(tout.at[2], join(e, parts_of(mown)))
+            send_t(2, to_last, 1).start()
+
+        enter_rows_of(e[1:3])
+        pieces(last_step, 0, SCORES_AT)
+
+    pass_rows(1 - core).wait_recv()
+    entering = jnp.concatenate(
+        [jnp.concatenate([vent[h, 0], vent[h, 1]], axis=1) for h in range(2)], axis=0
+    )
+    local_rows = jnp.zeros((head_rows, tokens), F32)
+    for t in range(tiles):
+        weight = jnp.broadcast_to(rd[t : t + 1, :], (head_rows, LANES)).astype(BF16)
+        local_rows = local_rows + mm_nt(weight, y[t].astype(BF16))
+    row_scores = []
+    for s in range(spans):
+        if s > 0:
+            entering = enter_rows[0][:, SPAN - 1 : SPAN] * entering + read_states[0]
+        far = mm_nt(entering.astype(BF16), c_ref[0, pl.ds(s * SPAN, SPAN), :]) * enter_rows[s]
+        far = jnp.sum(far, axis=0, keepdims=True)
+        row_scores.append(far + local_rows[0:1, s * SPAN : (s + 1) * SPAN])
+    row_scores = jnp.where(live_row, jnp.concatenate(row_scores, axis=1), 0.0)
+    for i in range(tokens // LANES):
+        sums[mine, i : i + 1, :] = row_scores[:, i * LANES : (i + 1) * LANES]
+
+    def score_copy(k):
+        return pltpu.make_async_remote_copy(
+            src_ref=sums.at[mine],
+            dst_ref=sums.at[mine],
+            send_sem=ysem_s.at[k],
+            recv_sem=ysem_r.at[k],
+            device_id={"head": lax.rem(mine + k, heads_axis)},
+            device_id_type=MESH,
+        )
+
+    for k in range(1, heads_axis):
+        score_copy(k).start()
+
+    @pl.when(chip >= 2)
+    def _():
+        pieces(last_step, SCORES_AT, half * steps)
+
+    def finish_tile(t):
         cols = pl.ds(pl.multiple_of(t * LANES, LANES), LANES)
         e0 = eown[t]
         e1 = (ta[t][0:1, :] * e0.astype(F32) + first[t]).astype(BF16)
-        parts = []
         for s, e in enumerate((e0, e1)):
             rows = pl.ds(s * SPAN, SPAN)
             enter = jnp.where(doc[rows, :] == 0.0, jnp.exp2(cum[t, rows, :]), 0.0)
             v = y[t, rows, :] + enter * mm(c_ref[0, rows, :], e)
             v = jnp.where(live[s * SPAN : (s + 1) * SPAN, :], v, 0.0).astype(BF16)
             out_ref[0, rows, cols] = v
-            parts.append(v)
-        v = jnp.concatenate(parts, axis=0)
-        weight = jnp.broadcast_to(read_ref[:, cols].astype(F32), (16, LANES)).astype(BF16)
-        return row_scores + mm_nt(weight, v)[0:8, :]
 
     for j in range(half):
-        row_scores = finish_tile(core * half + j, row_scores)
+        finish_tile(core * half + j)
     for j in range(half):
         for r in range(steps):
             piece = pl.ds(r * ROWS_STEP, ROWS_STEP)
@@ -271,23 +508,8 @@
                 device_id={"ctx": partner},
                 device_id_type=MESH,
             ).wait_recv()
-        row_scores = finish_tile((1 - core) * half + j, row_scores)
-
-    for i in range(tokens // LANES):
-        sums[mine, i : i + 1, :] = row_scores[0:1, i * LANES : (i + 1) * LANES]
-
-    def score_copy(k):
-        return pltpu.make_async_remote_copy(
-            src_ref=sums.at[mine],
-            dst_ref=sums.at[mine],
-            send_sem=ysem_s.at[k],
-            recv_sem=ysem_r.at[k],
-            device_id={"head": lax.rem(mine + k, heads_axis)},
-            device_id_type=MESH,
-        )
-
-    for k in range(1, heads_axis):
-        score_copy(k).start()
+        finish_tile((1 - core) * half + j)
+
     for k in range(1, heads_axis):
         score_copy(k).wait()
     total = sums[0]
@@ -298,13 +520,30 @@
 
     for j in range(half):
         state_copy(sbf, srecv, psem_s, psem_r, j, partner).wait_send()
-        for r in range(steps):
-            pass_copy(j, r).wait_send()
-
-            @pl.when(chip < last_chip)
-            def _():
-                chain_copy(j, r).wait_send()
     t_copy.wait_send()
+    pieces(lambda j, r: pass_copy(j, r).wait_send())
+
+    @pl.when(among(0, 2, 3, 4))
+    def _():
+        send_t(0, to_lead, 0).wait_send()
+        pieces(lambda j, r: send(outb.at[0], 0, j, r, to_lead, 0).wait_send())
+
+    pass_rows(core).wait_send()
+
+    @pl.when(among(1, 2, 5, 6))
+    def _():
+        send_t(1, to_join, join_slot).wait_send()
+        pieces(lambda j, r: send(outb.at[1], 1, j, r, to_join, join_slot).wait_send())
+
+    @pl.when(among(1, 3, 4, 7))
+    def _():
+        send_t(2, to_last, 1).wait_send()
+        pieces(lambda j, r: send(outb.at[2], 2, j, r, to_last, 1).wait_send())
+
+    @pl.when(chip == 1)
+    def _():
+        send_t(1, 2, 1, 3).wait_send()
+        pieces(lambda j, r: send(outb.at[1], 3, j, r, 2, 1).wait_send())
 
 
 def state_copy(src, dst, send, recv, j, partner):
@@ -349,27 +588,34 @@
             small(tiles),
             big(half, BF16),
             big(half, BF16),
-            small(half),
+            pltpu.VMEM((2, 4, 8, LANES), F32),
+            small(4),
+            small(4),
             big(half, F32),
-            small(half),
             big(half, F32),
-            small(half),
-            big(half, BF16),
-            big(half, BF16),
+            small(4),
+            small(4),
+            pltpu.VMEM((2, half, SPAN, LANES), BF16),
+            pltpu.VMEM((2, 4, 8, LANES), F32),
+            pltpu.VMEM((3, half, SPAN, LANES), BF16),
+            pltpu.VMEM((3, 4, 8, LANES), F32),
             big(tiles, BF16),
             big(half, BF16),
+            pltpu.VMEM((2, 2, 8, LANES), F32),
+            small(2),
             pltpu.VMEM((tiles, tokens, LANES), F32),
             pltpu.VMEM((spans, SPAN, SPAN), BF16),
             pltpu.VMEM((tokens // SUB, SUB, LANES), F32),
             pltpu.VMEM((heads_axis, tokens // LANES, LANES), F32),
+            pltpu.VMEM((tiles, LANES), F32),
             sem((half,)), sem((half,)), sem((2,)),
-            sem((half, steps)), sem((half, steps)),
-            sem((half, steps)), sem((half, steps)),
+            sem((4, half, steps)), sem((2, half, steps)), sem((4,)), sem((2,)),
+            sem((half, steps)), sem((half, steps)), sem((2,)),
             sem((heads_axis,)), sem((heads_axis,)),
         ],
         compiler_params=pltpu.CompilerParams(collective_id=0, has_side_effects=True),
         name="ssd",
-    )(counts, inputs, b_proj, c_proj, log_decay, starts, skip_gain, readout.reshape(1, width))
+    )(counts, inputs, b_proj, c_proj, log_decay, starts, skip_gain, readout.reshape(tiles, LANES))
 
 
 def solution(mesh):

time: 48.8 us -> 40.5 us (0.83)
  the two profiles are of different devices: /device:TPU:448 before, /device:TPU:130 now
where the time goes in v2:
time: 40.5 us; the launch traced here: 40.3 us
  Pallas kernels  36.2 us (89%)
  local copies, waits for them, and re-layouts  2.85 us (7%)
  between operations  1.3 us (3%)
    pallas_call x1, Pallas kernels, body(): pl.pallas_call(functools.partial(kernel, (ctxs, heads_axis, tokens, tiles...  36.2 us
    unnamed x4, local copies, waits for them, and re-layouts  2.85 us

profile of v2, /device:TPU:130, one launch (start us, length us, event | category | flops | bytes accessed | tf_op | source)
XLA Modules:
  0.0 40.3 jit_solution(14688061944436848222)
XLA Ops:
  1.3 36.2 %ssd.1 = (bf16[1,512,1024]{2,1,0:T(8,128)(2,1)}, f32[1,512]{1,0:T(1,128)}) custom-call(s32[1,1]{1,0:T(1,128)S(6)} %copy.12.count_ref, bf16[1,512,1024]{2,1,0:T(8,128)(2,1)} %x_ref.1, bf16[1,512,256]{2,1,0:T(8,128)(2,1)} %b_ref.1, bf16[1,512,256]{2,1,0:T(8,128)(2,1)} %c_ref.1, bf16[1,16,512]{2,1,0:T(8,128)(2,1)} %a_ref.1, s32[1,512]{1,0:T(1,128)} %s_ref.1, ...), custom_call_target="tpu_custom_call" | custom-call | tf_op jit(solution)/shard_map/ssd/pallas_call | solution.py:571
  37.5 0.0 copy-start
  37.5 2.3 %copy.13 = bf16[1,512,1024]{2,1,0:T(8,128)(2,1)} copy(bf16[1,512,1024]{2,1,0:T(8,128)(2,1)} %get-tuple-element.4) | data formatting | bytes 2097152
  39.7 0.0 copy-done
  39.7 0.6 %copy.14 = f32[1,512]{1,0:T(1,128)} copy(f32[1,512]{1,0:T(1,128)S(1)} %copy-done) | data formatting | bytes 4096
Async XLA Ops:
  37.5 2.3 %copy-start = (f32[1,512]{1,0:T(1,128)S(1)}, f32[1,512]{1,0:T(1,128)}, u32[]{:S(2)}) copy-start(f32[1,512]{1,0:T(1,128)} %get-tuple-element.5) | copy-start | bytes 6148

commit v3 on v2

--- a/solution.py
+++ b/solution.py
@@ -14,7 +14,8 @@
 LANES = 128
 ROWS_STEP = 64
 SCORES_AT = 6
-EDGES = ((0, 1), (1, 2), (2, 3), (1, 3), (1, 7), (3, 4), (4, 5), (5, 6), (6, 7))
+DIRECT = 4
+EDGES = ((0, 1), (1, 2), (2, 3), (1, 3), (1, 6), (1, 7), (3, 4), (3, 5), (4, 5), (5, 6), (6, 7))
 LOG2E = math.log2(math.e)
 F32 = jnp.float32
 BF16 = jnp.bfloat16
@@ -39,8 +40,9 @@
 
 def kernel(
     sizes,
-    count_ref, x_ref, b_ref, c_ref, a_ref, s_ref, gain_ref, read_ref,
+    count_ref, x_hbm, b_hbm, c_hbm, a_hbm, s_hbm, gain_ref, read_hbm,
     out_ref, score_ref,
+    x_ref, b_ref, c_ref, a_ref, s_ref, read_ref, isem,
     xm, lx, cum, doc, bt, first, whole, ta, td, sbf, srecv, mfull, msnd, mrecv,
     comb, base, mown, mbase, inb, tin, outb, tout, eown, psnd, vent, vsnd, y, gb, gm, sums, rd,
     psem_s, psem_r, tsem, csem_s, csem_r, vsem_s, vsem_r, fsem_s, fsem_r, wsem, ysem_s, ysem_r,
@@ -55,6 +57,14 @@
     mine = lax.axis_index("head")
     partner = ctx + 1 - 2 * core
 
+    loads = [
+        pltpu.make_async_copy(source, target, isem.at[i])
+        for i, (source, target) in enumerate(
+            ((a_hbm, a_ref), (s_hbm, s_ref), (read_hbm, read_ref), (b_hbm, b_ref), (x_hbm, x_ref), (c_hbm, c_ref))
+        )
+    ]
+    for load in loads:
+        load.start()
     barrier = pltpu.get_barrier_semaphore()
     pl.semaphore_signal(barrier, inc=1, device_id={"ctx": partner}, device_id_type=MESH)
     peers = heads_axis
@@ -75,6 +85,8 @@
 
     count = count_ref[0, 0]
     live_row = iota((1, tokens), 1) < count
+    loads[0].wait()
+    loads[1].wait()
     log_decay = jnp.where(live_row, a_ref[0].astype(F32), 0.0).astype(BF16)
     starts = jnp.where(live_row, s_ref[...].astype(F32), 0.0)
     head_rows = log_decay.shape[0]
@@ -89,7 +101,12 @@
         lx[rows, :] = mm_tn(log_decay[:, s * SPAN : (s + 1) * SPAN], spread).astype(BF16)
         spread_starts = mm_tn(starts[:, s * SPAN : (s + 1) * SPAN], ones).astype(BF16)
         doc[rows, :] = mm(tri, spread_starts)
+    loads[3].wait()
+    for s in range(spans):
+        rows = pl.ds(s * SPAN, SPAN)
         bt[:, rows] = b_ref[0, rows, :].astype(F32).T.astype(BF16)
+    loads[2].wait()
+    loads[4].wait()
 
     live = iota((tokens, LANES), 0) < count
 
@@ -204,13 +221,23 @@
             device_id_type=MESH,
         )
 
-    def send_t(out, to, slot, sem=None):
+    def send_t(out, to, slot):
         return pltpu.make_async_remote_copy(
             src_ref=tout.at[out],
             dst_ref=tin.at[slot],
-            send_sem=vsem_s.at[out if sem is None else sem],
+            send_sem=vsem_s.at[out],
             recv_sem=vsem_r.at[slot],
             device_id={"ctx": 2 * to + core},
+            device_id_type=MESH,
+        )
+
+    def back_t():
+        return pltpu.make_async_remote_copy(
+            src_ref=tin.at[1],
+            dst_ref=tin.at[1],
+            send_sem=vsem_s.at[3],
+            recv_sem=vsem_r.at[1],
+            device_id={"ctx": 4 + core},
             device_id_type=MESH,
         )
 
@@ -250,6 +277,7 @@
         )
 
     def local_part():
+        loads[5].wait()
         for s in range(spans):
             rows = pl.ds(s * SPAN, SPAN)
             scores = mm_nt(c_ref[0, rows, :], b_ref[0, rows, :])
@@ -377,6 +405,13 @@
         enter_rows_of((jnp.zeros((8, LANES), F32),) * 2)
         pieces(lambda j, r: enter(j, r, jnp.zeros((ROWS_STEP, LANES), F32)))
 
+    def direct(j, r, to):
+        @pl.when(j * steps + r >= half * steps - DIRECT)
+        def _():
+            send(outb.at[2], 3, j, r, to, 1).start()
+
+    rest = []
+
     @pl.when(chip == 1)
     def _():
         enter_rows_of((tin[0, 1], tin[0, 2]))
@@ -387,6 +422,7 @@
             got, own = inb[1, j, piece, :].astype(F32), outb[1, j, piece, :].astype(F32)
             outb[2, j, piece, :] = (row(tin.at[1], j) * own + got).astype(BF16)
             send(outb.at[2], 2, j, r, 7, 1).start()
+            direct(j, r, 6)
 
         def both(j, r):
             join_step(j, r)
@@ -398,10 +434,8 @@
         put(tout.at[2], join(parts_of(tout.at[1]), parts_of(tin.at[1])))
         send_t(2, 7, 1).start()
         pieces(both, behind, half * steps)
-        send_t(1, 2, 1, 3).start()
-        pieces(lambda j, r: send(outb.at[1], 3, j, r, 2, 1).start())
-        pieces(last_step, half * steps - behind, half * steps)
-        pieces(lambda j, r: enter(j, r, inb[0, j, rows_of(r), :].astype(F32)))
+        rest.append(lambda: pieces(last_step, half * steps - behind, half * steps))
+        rest.append(lambda: pieces(lambda j, r: enter(j, r, inb[0, j, rows_of(r), :].astype(F32))))
 
     joins = among(3, 5, 6, 7)
 
@@ -409,7 +443,7 @@
         piece = rows_of(r)
         send(outb.at[2], 2, j, r, 1, 1).wait_recv()
 
-        @pl.when(among(4, 7))
+        @pl.when(among(4, 7) & (j * steps + r < half * steps - DIRECT))
         def _():
             send(inb.at[1], 2, j, r, to_last, 1).start()
 
@@ -425,6 +459,8 @@
         def _():
             outb[2, j, piece, :] = (row(mown, j) * e + comb[j, piece, :]).astype(BF16)
             send(outb.at[2], 2, j, r, 4, 1).start()
+            direct(j, r, 5)
+            send(inb.at[1], 4, j, r, 2, 1).start()
 
         enter(j, r, e)
 
@@ -444,6 +480,7 @@
         def _():
             put(tout.at[2], join(e, parts_of(mown)))
             send_t(2, to_last, 1).start()
+            back_t().start()
 
         enter_rows_of(e[1:3])
         pieces(last_step, 0, SCORES_AT)
@@ -480,6 +517,11 @@
     for k in range(1, heads_axis):
         score_copy(k).start()
 
+    @pl.when(chip == 1)
+    def _():
+        for run in rest:
+            run()
+
     @pl.when(chip >= 2)
     def _():
         pieces(last_step, SCORES_AT, half * steps)
@@ -538,12 +580,21 @@
     @pl.when(among(1, 3, 4, 7))
     def _():
         send_t(2, to_last, 1).wait_send()
-        pieces(lambda j, r: send(outb.at[2], 2, j, r, to_last, 1).wait_send())
-
-    @pl.when(chip == 1)
-    def _():
-        send_t(1, 2, 1, 3).wait_send()
-        pieces(lambda j, r: send(outb.at[1], 3, j, r, 2, 1).wait_send())
+        pieces(lambda j, r: send(outb.at[2], 2, j, r, to_last, 1).wait_send(), 0, half * steps - DIRECT)
+
+    @pl.when(among(1, 3))
+    def _():
+        for out in (2, 3):
+            pieces(
+                lambda j, r: send(outb.at[2], out, j, r, 5, 1).wait_send(),
+                half * steps - DIRECT,
+                half * steps,
+            )
+
+    @pl.when(chip == 3)
+    def _():
+        back_t().wait_send()
+        pieces(lambda j, r: send(inb.at[1], 4, j, r, 2, 1).wait_send())
 
 
 def state_copy(src, dst, send, recv, j, partner):
@@ -565,6 +616,7 @@
     spans = tokens // SPAN
     steps = SPAN // ROWS_STEP
     vmem, smem = pl.BlockSpec(memory_space=pltpu.VMEM), pl.BlockSpec(memory_space=pltpu.SMEM)
+    hbm = pl.BlockSpec(memory_space=pltpu.HBM)
     big = lambda n, dtype: pltpu.VMEM((n, SPAN, LANES), dtype)
     small = lambda n: pltpu.VMEM((n, 8, LANES), F32)
     sem = pltpu.SemaphoreType.DMA
@@ -574,9 +626,16 @@
             jax.ShapeDtypeStruct(inputs.shape, BF16),
             jax.ShapeDtypeStruct((1, tokens), F32),
         ),
-        in_specs=[smem, vmem, vmem, vmem, vmem, vmem, smem, vmem],
+        in_specs=[smem, hbm, hbm, hbm, hbm, hbm, smem, hbm],
         out_specs=(vmem, vmem),
         scratch_shapes=[
+            pltpu.VMEM(inputs.shape, BF16),
+            pltpu.VMEM(b_proj.shape, BF16),
+            pltpu.VMEM(c_proj.shape, BF16),
+            pltpu.VMEM(log_decay.shape, BF16),
+            pltpu.VMEM(starts.shape, starts.dtype),
+            pltpu.VMEM((tiles, LANES), BF16),
+            sem((6,)),
             pltpu.VMEM((tiles, tokens, LANES), BF16),
             pltpu.VMEM((tokens, width), BF16),
             pltpu.VMEM((tiles, tokens, LANES), F32),
@@ -609,7 +668,7 @@
             pltpu.VMEM((heads_axis, tokens // LANES, LANES), F32),
             pltpu.VMEM((tiles, LANES), F32),
             sem((half,)), sem((half,)), sem((2,)),
-            sem((4, half, steps)), sem((2, half, steps)), sem((4,)), sem((2,)),
+            sem((5, half, steps)), sem((2, half, steps)), sem((4,)), sem((2,)),
             sem((half, steps)), sem((half, steps)), sem((2,)),
             sem((heads_axis,)), sem((heads_axis,)),
         ],

time: 40.5 us -> 37.7 us (0.931)
  the two profiles are of different devices: /device:TPU:130 before, /device:TPU:324 now
where the time goes in v3:
time: 37.7 us; the launch traced here: 37.5 us
  Pallas kernels  33.3 us (88%)
  local copies, waits for them, and re-layouts  2.85 us (8%)
  between operations  1.3 us (3%)
    pallas_call x1, Pallas kernels, body(): pl.pallas_call(functools.partial(kernel, (ctxs, heads_axis, tokens, tiles...  33.3 us
    unnamed x4, local copies, waits for them, and re-layouts  2.85 us

profile of v3, /device:TPU:324, one launch (start us, length us, event | category | flops | bytes accessed | tf_op | source)
XLA Modules:
  0.0 37.5 jit_solution(12454446332524707847)
XLA Ops:
  1.3 33.3 %ssd.1 = (bf16[1,512,1024]{2,1,0:T(8,128)(2,1)}, f32[1,512]{1,0:T(1,128)}) custom-call(s32[1,1]{1,0:T(1,128)S(6)} %copy.12.count_ref, bf16[1,512,1024]{2,1,0:T(8,128)(2,1)} %x_hbm.1, bf16[1,512,256]{2,1,0:T(8,128)(2,1)} %b_hbm.1, bf16[1,512,256]{2,1,0:T(8,128)(2,1)} %c_hbm.1, bf16[1,16,512]{2,1,0:T(8,128)(2,1)} %a_hbm.1, s32[1,512]{1,0:T(1,128)} %s_hbm.1, ...), custom_call_target="tpu_custom_call" | custom-call | tf_op jit(solution)/shard_map/ssd/pallas_call | solution.py:623
  34.6 0.0 copy-start
  34.6 2.3 %copy.13 = bf16[1,512,1024]{2,1,0:T(8,128)(2,1)} copy(bf16[1,512,1024]{2,1,0:T(8,128)(2,1)} %get-tuple-element.4) | data formatting | bytes 2097152
  36.9 0.0 copy-done
  36.9 0.6 %copy.14 = f32[1,512]{1,0:T(1,128)} copy(f32[1,512]{1,0:T(1,128)S(1)} %copy-done) | data formatting | bytes 4096
Async XLA Ops:
  34.6 2.3 %copy-start = (f32[1,512]{1,0:T(1,128)S(1)}, f32[1,512]{1,0:T(1,128)}, u32[]{:S(2)}) copy-start(f32[1,512]{1,0:T(1,128)} %get-tuple-element.5) | copy-start | bytes 6148

commit v4 on v3

--- a/solution.py
+++ b/solution.py
@@ -41,11 +41,12 @@
 def kernel(
     sizes,
     count_ref, x_hbm, b_hbm, c_hbm, a_hbm, s_hbm, gain_ref, read_hbm,
-    out_ref, score_ref,
+    out_hbm, score_ref,
+    out_ref, osem,
     x_ref, b_ref, c_ref, a_ref, s_ref, read_ref, isem,
     xm, lx, cum, doc, bt, first, whole, ta, td, sbf, srecv, mfull, msnd, mrecv,
     comb, base, mown, mbase, inb, tin, outb, tout, eown, psnd, vent, vsnd, y, gb, gm, sums, rd,
-    psem_s, psem_r, tsem, csem_s, csem_r, vsem_s, vsem_r, fsem_s, fsem_r, wsem, ysem_s, ysem_r,
+    psem_s, psem_r, tsem, csem_s, csem_r, vsem_s, vsem_r, fsem_s, fsem_r, wsem, ready, yready, ysem_s, ysem_r,
 ):
     ctxs, heads_axis, tokens, tiles = sizes
     half = tiles // 2
@@ -66,22 +67,27 @@
     for load in loads:
         load.start()
     barrier = pltpu.get_barrier_semaphore()
+    middle = heads_axis // 2
+
+    def rank(i):
+        return jnp.where(i < middle, i, heads_axis + middle - 1 - i)
+
+    others = [lax.rem(mine + k, heads_axis) for k in range(heads_axis)]
     pl.semaphore_signal(barrier, inc=1, device_id={"ctx": partner}, device_id_type=MESH)
-    peers = heads_axis
-    for ends in EDGES:
-        for here, there in (ends, ends[::-1]):
-            peers = peers + jnp.where(chip == here, 1, 0)
-
-            @pl.when(chip == here)
-            def _():
-                pl.semaphore_signal(
-                    barrier, inc=1, device_id={"ctx": 2 * there + core}, device_id_type=MESH
-                )
-
-    for k in range(1, heads_axis):
-        pl.semaphore_signal(
-            barrier, inc=1, device_id={"head": lax.rem(mine + k, heads_axis)}, device_id_type=MESH
-        )
+    peers = 1 + rank(mine)
+    for here, there in EDGES:
+        peers = peers + jnp.where(chip == there, 1, 0)
+
+        @pl.when(chip == here)
+        def _():
+            pl.semaphore_signal(
+                barrier, inc=1, device_id={"ctx": 2 * there + core}, device_id_type=MESH
+            )
+
+    for other in others[1:]:
+        @pl.when(rank(other) > rank(mine))
+        def _():
+            pl.semaphore_signal(barrier, inc=1, device_id={"head": other}, device_id_type=MESH)
 
     count = count_ref[0, 0]
     live_row = iota((1, tokens), 1) < count
@@ -110,6 +116,26 @@
 
     live = iota((tokens, LANES), 0) < count
 
+    pl.semaphore_wait(barrier, peers)
+    for here, there in EDGES:
+        if (here, there) != (1, 2):
+            @pl.when(chip == there)
+            def _():
+                pl.semaphore_signal(
+                    ready.at[there], inc=1, device_id={"ctx": 2 * here + core}, device_id_type=MESH
+                )
+
+    for other in others[1:]:
+        @pl.when(rank(other) < rank(mine))
+        def _():
+            pl.semaphore_signal(yready, inc=1, device_id={"head": other}, device_id_type=MESH)
+
+    def meet(here, *there):
+        @pl.when(chip == here)
+        def _():
+            for other in there:
+                pl.semaphore_wait(ready.at[other], 1)
+
     rd[...] = read_ref[...].astype(F32)
     upper = jnp.where(iota((SPAN, SPAN), 0) <= iota((SPAN, SPAN), 1), 1.0, 0.0).astype(BF16)
     head_of = iota((head_rows, LANES), 1) // SUB
@@ -159,8 +185,6 @@
 
     for j in range(half):
         sbf[j] = state_tile((1 - core) * half + j).astype(BF16)
-        if j == 0:
-            pl.semaphore_wait(barrier, peers)
         state_copy(sbf, srecv, psem_s, psem_r, j, partner).start()
     t_copy = pltpu.make_async_remote_copy(
         src_ref=msnd,
@@ -334,6 +358,10 @@
 
         lax.fori_loop(0, tiles, tile, 0)
 
+    meet(0, 1)
+    meet(2, 3)
+    meet(4, 5)
+
     @pl.when(among(0, 2, 3, 4))
     def _():
         tout[0] = mown[...]
@@ -347,6 +375,9 @@
         pieces(step)
 
     local_part()
+    meet(1, 3)
+    meet(5, 6)
+    meet(6, 7)
 
     @pl.when(among(1, 2, 3, 5, 6, 7))
     def _():
@@ -362,6 +393,13 @@
         got, own = parts_of(tin.at[0]), parts_of(mown)
         put(tout.at[1], join(pick(is_later, own, got), pick(is_later, got, own)))
         send_t(1, to_join, join_slot).start()
+
+    def enter(j, r, e):
+        piece = rows_of(r)
+        f = row(mbase, j) * e + base[j, piece, :]
+        eown[core * half + j, piece, :] = jnp.where(is_low, e, f).astype(BF16)
+        psnd[j, piece, :] = jnp.where(is_low, f, e).astype(BF16)
+        pass_copy(j, r).start()
 
     def join_step(j, r):
         piece = rows_of(r)
@@ -372,16 +410,13 @@
         outb[1, j, piece, :] = joined.astype(BF16)
         send(outb.at[1], 1, j, r, to_join, join_slot).start()
 
+        @pl.when(chip == 1)
+        def _():
+            enter(j, r, got)
+
     @pl.when(among(2, 5, 6))
     def _():
         pieces(join_step)
-
-    def enter(j, r, e):
-        piece = rows_of(r)
-        f = row(mbase, j) * e + base[j, piece, :]
-        eown[core * half + j, piece, :] = jnp.where(is_low, e, f).astype(BF16)
-        psnd[j, piece, :] = jnp.where(is_low, f, e).astype(BF16)
-        pass_copy(j, r).start()
 
     def pass_rows(side):
         return pltpu.make_async_remote_copy(
@@ -431,11 +466,11 @@
         behind = (half // 2) * steps
         pieces(join_step, 0, behind)
         send_t(1, 1, 1).wait_recv()
+        meet(1, 6, 7)
         put(tout.at[2], join(parts_of(tout.at[1]), parts_of(tin.at[1])))
         send_t(2, 7, 1).start()
         pieces(both, behind, half * steps)
         rest.append(lambda: pieces(last_step, half * steps - behind, half * steps))
-        rest.append(lambda: pieces(lambda j, r: enter(j, r, inb[0, j, rows_of(r), :].astype(F32))))
 
     joins = among(3, 5, 6, 7)
 
@@ -467,6 +502,7 @@
     @pl.when(chip >= 2)
     def _():
         send_t(2, 1, 1).wait_recv()
+        meet(3, 4, 5)
 
         @pl.when(among(4, 7))
         def _():
@@ -514,6 +550,10 @@
             device_id_type=MESH,
         )
 
+    @pl.when(rank(mine) < heads_axis - 1)
+    def _():
+        pl.semaphore_wait(yready, heads_axis - 1 - rank(mine))
+
     for k in range(1, heads_axis):
         score_copy(k).start()
 
@@ -525,6 +565,13 @@
     @pl.when(chip >= 2)
     def _():
         pieces(last_step, SCORES_AT, half * steps)
+
+    def out_copy(t):
+        return pltpu.make_async_copy(
+            out_ref.at[t],
+            out_hbm.at[0, :, pl.ds(pl.multiple_of(t * LANES, LANES), LANES)],
+            osem.at[t],
+        )
 
     def finish_tile(t):
         cols = pl.ds(pl.multiple_of(t * LANES, LANES), LANES)
@@ -535,7 +582,8 @@
             enter = jnp.where(doc[rows, :] == 0.0, jnp.exp2(cum[t, rows, :]), 0.0)
             v = y[t, rows, :] + enter * mm(c_ref[0, rows, :], e)
             v = jnp.where(live[s * SPAN : (s + 1) * SPAN, :], v, 0.0).astype(BF16)
-            out_ref[0, rows, cols] = v
+            out_ref[t, rows, :] = v
+        out_copy(t).start()
 
     for j in range(half):
         finish_tile(core * half + j)
@@ -560,6 +608,8 @@
     for i in range(tokens // LANES):
         score_ref[:, i * LANES : (i + 1) * LANES] = total[i : i + 1, :]
 
+    for t in range(tiles):
+        out_copy(t).wait()
     for j in range(half):
         state_copy(sbf, srecv, psem_s, psem_r, j, partner).wait_send()
     t_copy.wait_send()
@@ -627,8 +677,10 @@
             jax.ShapeDtypeStruct((1, tokens), F32),
         ),
         in_specs=[smem, hbm, hbm, hbm, hbm, hbm, smem, hbm],
-        out_specs=(vmem, vmem),
+        out_specs=(pl.BlockSpec(memory_space=pltpu.HBM), vmem),
         scratch_shapes=[
+            pltpu.VMEM((tiles, tokens, LANES), BF16),
+            sem((tiles,)),
             pltpu.VMEM(inputs.shape, BF16),
             pltpu.VMEM(b_proj.shape, BF16),
             pltpu.VMEM(c_proj.shape, BF16),
@@ -670,6 +722,7 @@
             sem((half,)), sem((half,)), sem((2,)),
             sem((5, half, steps)), sem((2, half, steps)), sem((4,)), sem((2,)),
             sem((half, steps)), sem((half, steps)), sem((2,)),
+            pltpu.SemaphoreType.REGULAR((ctxs // 2,)), pltpu.SemaphoreType.REGULAR,
             sem((heads_axis,)), sem((heads_axis,)),
         ],
         compiler_params=pltpu.CompilerParams(collective_id=0, has_side_effects=True),

time: 37.7 us -> 36.2 us (0.960)
  the two profiles are of different devices: /device:TPU:324 before, /device:TPU:384 now
where the time goes in v4:
time: 36.2 us; the launch traced here: 36 us
  Pallas kernels  31.8 us (88%)
  local copies, waits for them, and re-layouts  2.85 us (8%)
  between operations  1.3 us (4%)
    pallas_call x1, Pallas kernels, body(): pl.pallas_call(functools.partial(kernel, (ctxs, heads_axis, tokens, tiles...  31.8 us
    unnamed x4, local copies, waits for them, and re-layouts  2.85 us

profile of v4, /device:TPU:384, one launch (start us, length us, event | category | flops | bytes accessed | tf_op | source)
XLA Modules:
  0.0 36.0 jit_solution(17021166426242957460)
XLA Ops:
  1.3 31.8 %ssd.1 = (bf16[1,512,1024]{2,1,0:T(8,128)(2,1)}, f32[1,512]{1,0:T(1,128)}) custom-call(s32[1,1]{1,0:T(1,128)S(6)} %copy.12.count_ref, bf16[1,512,1024]{2,1,0:T(8,128)(2,1)} %x_hbm.1, bf16[1,512,256]{2,1,0:T(8,128)(2,1)} %b_hbm.1, bf16[1,512,256]{2,1,0:T(8,128)(2,1)} %c_hbm.1, bf16[1,16,512]{2,1,0:T(8,128)(2,1)} %a_hbm.1, s32[1,512]{1,0:T(1,128)} %s_hbm.1, ...), custom_call_target="tpu_custom_call" | custom-call | tf_op jit(solution)/shard_map/ssd/pallas_call | solution.py:673
  33.1 0.0 copy-start
  33.1 2.3 %copy.13 = bf16[1,512,1024]{2,1,0:T(8,128)(2,1)} copy(bf16[1,512,1024]{2,1,0:T(8,128)(2,1)} %get-tuple-element.4) | data formatting | bytes 2097152
  35.4 0.0 copy-done
  35.4 0.6 %copy.14 = f32[1,512]{1,0:T(1,128)} copy(f32[1,512]{1,0:T(1,128)S(1)} %copy-done) | data formatting | bytes 4096
Async XLA Ops:
  33.1 2.3 %copy-start = (f32[1,512]{1,0:T(1,128)S(1)}, f32[1,512]{1,0:T(1,128)}, u32[]{:S(2)}) copy-start(f32[1,512]{1,0:T(1,128)} %get-tuple-element.5) | copy-start | bytes 6148

commit v5 on v4

--- a/solution.py
+++ b/solution.py
@@ -13,8 +13,8 @@
 SUB = 64
 LANES = 128
 ROWS_STEP = 64
-SCORES_AT = 6
-DIRECT = 4
+SCORES_AT = 3
+DIRECT = 6
 EDGES = ((0, 1), (1, 2), (2, 3), (1, 3), (1, 6), (1, 7), (3, 4), (3, 5), (4, 5), (5, 6), (6, 7))
 LOG2E = math.log2(math.e)
 F32 = jnp.float32
@@ -118,12 +118,11 @@
 
     pl.semaphore_wait(barrier, peers)
     for here, there in EDGES:
-        if (here, there) != (1, 2):
-            @pl.when(chip == there)
-            def _():
-                pl.semaphore_signal(
-                    ready.at[there], inc=1, device_id={"ctx": 2 * here + core}, device_id_type=MESH
-                )
+        @pl.when(chip == there)
+        def _():
+            pl.semaphore_signal(
+                ready.at[there], inc=1, device_id={"ctx": 2 * here + core}, device_id_type=MESH
+            )
 
     for other in others[1:]:
         @pl.when(rank(other) < rank(mine))
@@ -375,7 +374,7 @@
         pieces(step)
 
     local_part()
-    meet(1, 3)
+    meet(1, 2, 3)
     meet(5, 6)
     meet(6, 7)
 
@@ -470,6 +469,7 @@
         put(tout.at[2], join(parts_of(tout.at[1]), parts_of(tin.at[1])))
         send_t(2, 7, 1).start()
         pieces(both, behind, half * steps)
+        pieces(lambda j, r: send(outb.at[1], 4, j, r, 2, 1).start(), half * steps - DIRECT, half * steps)
         rest.append(lambda: pieces(last_step, half * steps - behind, half * steps))
 
     joins = among(3, 5, 6, 7)
@@ -495,7 +495,10 @@
             outb[2, j, piece, :] = (row(mown, j) * e + comb[j, piece, :]).astype(BF16)
             send(outb.at[2], 2, j, r, 4, 1).start()
             direct(j, r, 5)
-            send(inb.at[1], 4, j, r, 2, 1).start()
+
+            @pl.when(j * steps + r < half * steps - DIRECT)
+            def _():
+                send(inb.at[1], 4, j, r, 2, 1).start()
 
         enter(j, r, e)
 
@@ -644,7 +647,15 @@
     @pl.when(chip == 3)
     def _():
         back_t().wait_send()
-        pieces(lambda j, r: send(inb.at[1], 4, j, r, 2, 1).wait_send())
+        pieces(lambda j, r: send(inb.at[1], 4, j, r, 2, 1).wait_send(), 0, half * steps - DIRECT)
+
+    @pl.when(chip == 1)
+    def _():
+        pieces(
+            lambda j, r: send(outb.at[1], 4, j, r, 2, 1).wait_send(),
+            half * steps - DIRECT,
+            half * steps,
+        )
 
 
 def state_copy(src, dst, send, recv, j, partner):

time: 36.2 us -> 34.2 us (0.945)
  the two profiles are of different devices: /device:TPU:384 before, /device:TPU:64 now
where the time goes in v5:
time: 34.2 us; the launch traced here: 34 us
  Pallas kernels  29.8 us (87%)
  local copies, waits for them, and re-layouts  2.85 us (8%)
  between operations  1.3 us (4%)
    pallas_call x1, Pallas kernels, body(): pl.pallas_call(functools.partial(kernel, (ctxs, heads_axis, tokens, tiles...  29.8 us
    unnamed x4, local copies, waits for them, and re-layouts  2.85 us

profile of v5, /device:TPU:64, one launch (start us, length us, event | category | flops | bytes accessed | tf_op | source)
XLA Modules:
  0.0 34.0 jit_solution(5375642965264097707)
XLA Ops:
  1.3 29.8 %ssd.1 = (bf16[1,512,1024]{2,1,0:T(8,128)(2,1)}, f32[1,512]{1,0:T(1,128)}) custom-call(s32[1,1]{1,0:T(1,128)S(6)} %copy.12.count_ref, bf16[1,512,1024]{2,1,0:T(8,128)(2,1)} %x_hbm.1, bf16[1,512,256]{2,1,0:T(8,128)(2,1)} %b_hbm.1, bf16[1,512,256]{2,1,0:T(8,128)(2,1)} %c_hbm.1, bf16[1,16,512]{2,1,0:T(8,128)(2,1)} %a_hbm.1, s32[1,512]{1,0:T(1,128)} %s_hbm.1, ...), custom_call_target="tpu_custom_call" | custom-call | tf_op jit(solution)/shard_map/ssd/pallas_call | solution.py:684
  31.1 0.0 copy-start
  31.1 2.3 %copy.13 = bf16[1,512,1024]{2,1,0:T(8,128)(2,1)} copy(bf16[1,512,1024]{2,1,0:T(8,128)(2,1)} %get-tuple-element.4) | data formatting | bytes 2097152
  33.4 0.0 copy-done
  33.4 0.6 %copy.14 = f32[1,512]{1,0:T(1,128)} copy(f32[1,512]{1,0:T(1,128)S(1)} %copy-done) | data formatting | bytes 4096
Async XLA Ops:
  31.1 2.3 %copy-start = (f32[1,512]{1,0:T(1,128)S(1)}, f32[1,512]{1,0:T(1,128)}, u32[]{:S(2)}) copy-start(f32[1,512]{1,0:T(1,128)} %get-tuple-element.5) | copy-start | bytes 6148

commit v6 on v5

--- a/solution.py
+++ b/solution.py
@@ -135,6 +135,31 @@
             for other in there:
                 pl.semaphore_wait(ready.at[other], 1)
 
+    def state_tile(t):
+        cols = pl.ds(pl.multiple_of(t * LANES, LANES), LANES)
+        xt = jnp.where(live, x_ref[0, :, cols].astype(F32), 0.0).astype(BF16)
+        xm[t] = xt
+        states, totals = [], []
+        for s in range(spans):
+            rows = slice(s * SPAN, (s + 1) * SPAN)
+            run = mm(tri, lx[pl.ds(s * SPAN, SPAN), cols]) * LOG2E
+            cum[t, pl.ds(s * SPAN, SPAN), :] = run
+            docs = doc[pl.ds(s * SPAN, SPAN), :]
+            last = run[SPAN - 1 : SPAN, :]
+            keep = jnp.where(docs == docs[SPAN - 1 : SPAN, :], jnp.exp2(last - run), 0.0)
+            weighted = (xt[rows, :].astype(F32) * keep).astype(BF16)
+            states.append(mm(bt[:, pl.ds(s * SPAN, SPAN)], weighted))
+            totals.append(jnp.where(docs[SPAN - 1 : SPAN, :] == 0.0, jnp.exp2(last), 0.0))
+        first[t] = states[0]
+        joined = totals[1] * states[0] + states[1]
+        whole[t] = joined
+        ta[t] = jnp.broadcast_to(totals[0], (8, LANES))
+        td[t] = jnp.broadcast_to(totals[0] * totals[1], (8, LANES))
+        return joined
+
+    for j in range(half):
+        sbf[j] = state_tile((1 - core) * half + j).astype(BF16)
+        state_copy(sbf, srecv, psem_s, psem_r, j, partner).start()
     rd[...] = read_ref[...].astype(F32)
     upper = jnp.where(iota((SPAN, SPAN), 0) <= iota((SPAN, SPAN), 1), 1.0, 0.0).astype(BF16)
     head_of = iota((head_rows, LANES), 1) // SUB
@@ -160,31 +185,6 @@
             mfull[h, 1 + i] = read_state[rows, i * LANES : (i + 1) * LANES]
         mfull[h, 3] = row_totals[0][rows] * row_totals[1][rows]
 
-    def state_tile(t):
-        cols = pl.ds(pl.multiple_of(t * LANES, LANES), LANES)
-        xt = jnp.where(live, x_ref[0, :, cols].astype(F32), 0.0).astype(BF16)
-        xm[t] = xt
-        states, totals = [], []
-        for s in range(spans):
-            rows = slice(s * SPAN, (s + 1) * SPAN)
-            run = mm(tri, lx[pl.ds(s * SPAN, SPAN), cols]) * LOG2E
-            cum[t, pl.ds(s * SPAN, SPAN), :] = run
-            docs = doc[pl.ds(s * SPAN, SPAN), :]
-            last = run[SPAN - 1 : SPAN, :]
-            keep = jnp.where(docs == docs[SPAN - 1 : SPAN, :], jnp.exp2(last - run), 0.0)
-            weighted = (xt[rows, :].astype(F32) * keep).astype(BF16)
-            states.append(mm(bt[:, pl.ds(s * SPAN, SPAN)], weighted))
-            totals.append(jnp.where(docs[SPAN - 1 : SPAN, :] == 0.0, jnp.exp2(last), 0.0))
-        first[t] = states[0]
-        joined = totals[1] * states[0] + states[1]
-        whole[t] = joined
-        ta[t] = jnp.broadcast_to(totals[0], (8, LANES))
-        td[t] = jnp.broadcast_to(totals[0] * totals[1], (8, LANES))
-        return joined
-
-    for j in range(half):
-        sbf[j] = state_tile((1 - core) * half + j).astype(BF16)
-        state_copy(sbf, srecv, psem_s, psem_r, j, partner).start()
     t_copy = pltpu.make_async_remote_copy(
         src_ref=msnd,
         dst_ref=mrecv,

time: 34.2 us -> 34.6 us (1.012)
  the two profiles are of different devices: /device:TPU:64 before, /device:TPU:384 now
where the time goes in v6:
time: 34.6 us; the launch traced here: 34.4 us
  Pallas kernels  30.3 us (88%)
  local copies, waits for them, and re-layouts  2.85 us (8%)
  between operations  1.3 us (4%)
    pallas_call x1, Pallas kernels, body(): pl.pallas_call(functools.partial(kernel, (ctxs, heads_axis, tokens, tiles...  30.3 us
    unnamed x4, local copies, waits for them, and re-layouts  2.85 us

profile of v6, /device:TPU:384, one launch (start us, length us, event | category | flops | bytes accessed | tf_op | source)
XLA Modules:
  0.0 34.4 jit_solution(14169796791227563514)
XLA Ops:
  1.3 30.3 %ssd.1 = (bf16[1,512,1024]{2,1,0:T(8,128)(2,1)}, f32[1,512]{1,0:T(1,128)}) custom-call(s32[1,1]{1,0:T(1,128)S(6)} %copy.12.count_ref, bf16[1,512,1024]{2,1,0:T(8,128)(2,1)} %x_hbm.1, bf16[1,512,256]{2,1,0:T(8,128)(2,1)} %b_hbm.1, bf16[1,512,256]{2,1,0:T(8,128)(2,1)} %c_hbm.1, bf16[1,16,512]{2,1,0:T(8,128)(2,1)} %a_hbm.1, s32[1,512]{1,0:T(1,128)} %s_hbm.1, ...), custom_call_target="tpu_custom_call" | custom-call | tf_op jit(solution)/shard_map/ssd/pallas_call | solution.py:684
  31.5 0.0 copy-start
  31.6 2.3 %copy.13 = bf16[1,512,1024]{2,1,0:T(8,128)(2,1)} copy(bf16[1,512,1024]{2,1,0:T(8,128)(2,1)} %get-tuple-element.4) | data formatting | bytes 2097152
  33.8 0.0 copy-done
  33.8 0.6 %copy.14 = f32[1,512]{1,0:T(1,128)} copy(f32[1,512]{1,0:T(1,128)S(1)} %copy-done) | data formatting | bytes 4096
Async XLA Ops:
  31.5 2.3 %copy-start = (f32[1,512]{1,0:T(1,128)S(1)}, f32[1,512]{1,0:T(1,128)}, u32[]{:S(2)}) copy-start(f32[1,512]{1,0:T(1,128)} %get-tuple-element.5) | copy-start | bytes 6148
